TPU v7x, 256 devices: a whole 4x4x8 slice. The times are simulated.
256 devices in a mesh: gz: 8 (over x, core), gy: 32 (over y, z).
Axes of the slice: x: 4, y: 4, z: 8, core: 2. Of those that a mesh axis runs over, the one named last changes fastest.
Arguments:
- zone_ids: int32 [64, 1024, 512], P('gz', 'gy'), may hold values from 0 to 7
- fixed_cells: int32 [64, 1024, 512], P('gz', 'gy'), may hold values 0 or 1
- pressure_old: float32 [64, 1024, 512], P('gz', 'gy'), may hold values from -6 to 6
- pressure_iter: float32 [64, 1024, 512], P('gz', 'gy'), may hold values from -6 to 6
- strain_change: float32 [64, 1024, 512], P('gz', 'gy'), may hold values from -3 to 3
- source: float32 [64, 1024, 512], P('gz', 'gy'), may hold values from -40 to 40
- zone_perm: float32 [8], replicated, may hold values from 0.2 to 5
- zone_storage: float32 [8], replicated, may hold values from 0.1 to 1
- zone_biot: float32 [8], replicated, may hold values from 0.5 to 1
- zone_bulk: float32 [8], replicated, may hold values from 0.5 to 2
Outputs:
- pressure: float32 [64, 1024, 512], P('gz', 'gy')
- strain_next: float32 [64, 1024, 512], P('gz', 'gy')
- outer_norms: float32 [2], replicated
All inputs are finite; a program needn't handle non-finite values. No bound on the sum of `fixed_cells` on one device may be relied on, other than what follows from the above.
Results may differ from a plain program's by a relative error of at most 0.00016.
Values sent between devices are 32-bit elements; how exact they have to be, the bound alone decides.
A program may use at most 64 MiB of HBM per device.

v0:
```python
import jax
import jax.numpy as jnp
from jax import lax
from jax.sharding import Mesh
from jax.sharding import PartitionSpec as P

ITERS = 3
GZ = ("gz_0", "gz_1")
GY = ("gy_0", "gy_1")


def copy_for_each(array, axis):
    size = lax.axis_size(axis)
    return lax.all_to_all(
        jnp.broadcast_to(array[None], (size, *array.shape)), axis, 0, 0, tiled=True
    )


def of_everyone(array, axis):
    return copy_for_each(array, axis).sum(axis=0)


def one_axis_at_a_time(array, axes):
    far, near = axes
    nearer = of_everyone(array, near)
    return of_everyone(nearer, far)


def in_one(arrays, axis):
    line, at, outs = (jnp.concatenate([a.reshape(-1) for a in arrays]), 0, [])
    subtotal = one_axis_at_a_time(line, axis)
    for a in arrays:
        outs.append(subtotal[at : at + a.size].reshape(a.shape))
        at += a.size
    return tuple(outs)


def with_halo(array, sides, width):
    edges = {}
    for axis, dim in sides:
        size, length = (lax.axis_size(axis), array.shape[dim])
        up = [(i, (i + 1) % size) for i in range(size - 1)]
        last = lax.slice_in_dim(array, length - width, length, axis=dim)
        first = lax.slice_in_dim(array, 0, width, axis=dim)
        edges[dim] = (
            lax.ppermute(last, axis, up),
            lax.ppermute(first, axis, [(b, a) for a, b in up]),
        )
    done = []
    for _, dim in sides:
        low, high = edges[dim]
        around = [(width, width) if d in done else (0, 0) for d in range(array.ndim)]
        array = jnp.concatenate([jnp.pad(low, around), array, jnp.pad(high, around)], axis=dim)
        done.append(dim)
    return array


def lookup(zone_ids, zone_table):
    result = jnp.zeros(zone_ids.shape, jnp.float32)
    for zone_index in range(zone_table.shape[0]):
        result = jnp.where(zone_ids == zone_index, zone_table[zone_index], result)
    return result


def harmonic(lower_side, upper_side):
    return 2.0 * lower_side * upper_side / (lower_side + upper_side)


def neighbour_views(values, padded):
    x_padded = jnp.pad(values, ((0, 0), (0, 0), (1, 1)))
    return (
        padded[:-2, 1:-1],
        padded[2:, 1:-1],
        padded[1:-1, :-2],
        padded[1:-1, 2:],
        x_padded[:, :, :-2],
        x_padded[:, :, 2:],
    )


def paired_totals(residual, precond, applied):
    return in_one(
        (jnp.sum(residual * precond), jnp.sum(precond * applied)),
        (("gz_0", "gz_1"), ("gy_0", "gy_1")),
    )


def per_device(
    zone_ids,
    fixed_cells,
    pressure_old,
    pressure_iter,
    strain_change,
    source,
    zone_perm,
    zone_storage,
    zone_biot,
    zone_bulk,
):
    storage = lookup(zone_ids, zone_storage)
    biot_coeff = lookup(zone_ids, zone_biot)
    bulk_modulus = lookup(zone_ids, zone_bulk)
    permeability = lookup(zone_ids, zone_perm)
    coupling = biot_coeff * biot_coeff / bulk_modulus
    perm_padded = with_halo(permeability, ((GZ, 0), (GY, 1)), 1)
    face_terms = tuple(
        (harmonic(permeability, view) for view in neighbour_views(permeability, perm_padded))
    )
    diagonal = storage + coupling
    for face in face_terms:
        diagonal = diagonal + face
    free_cells = 1.0 - fixed_cells.astype(jnp.float32)
    cell_count = zone_ids.size * lax.axis_size(GZ) * lax.axis_size(GY)

    def operator(values):
        padded = with_halo(values, ((GZ, 0), (GY, 1)), 1)
        views = neighbour_views(values, padded)
        neighbours = face_terms[0] * views[0]
        for number in range(1, 6):
            neighbours = neighbours + face_terms[number] * views[number]
        return diagonal * values - neighbours

    right_side = (
        storage * pressure_old + coupling * pressure_iter - biot_coeff * strain_change + source
    )
    pressure = pressure_iter
    residual = free_cells * (right_side - operator(pressure_iter))
    precond = residual / diagonal
    applied = free_cells * operator(precond)
    inner_now, curvature = paired_totals(residual, precond, applied)
    step_size = inner_now / curvature
    direction = precond
    direction_image = applied
    for step_index in range(ITERS):
        pressure = pressure + step_size * direction
        residual = residual - step_size * direction_image
        if step_index + 1 < ITERS:
            precond = residual / diagonal
            applied = free_cells * operator(precond)
            inner_next, curvature = paired_totals(residual, precond, applied)
            growth = inner_next / inner_now
            step_size = inner_next / (curvature - growth * inner_next / step_size)
            direction = precond + growth * direction
            direction_image = applied + growth * direction_image
            inner_now = inner_next
    change = biot_coeff / bulk_modulus * (pressure - pressure_iter)
    strain_next = strain_change + change
    totals = in_one(
        (jnp.sum(residual * residual), jnp.sum(change * change)),
        (("gz_0", "gz_1"), ("gy_0", "gy_1")),
    )
    outer_norms = jnp.sqrt(jnp.stack([totals[0], totals[1]]) / cell_count)
    return (pressure, strain_next, outer_norms)


def solution(mesh):
    finer = Mesh(mesh.devices.reshape(4, 2, 4, 8), ("gz_0", "gz_1", "gy_0", "gy_1"))
    placed = (
        P(GZ, GY, None),
        P(GZ, GY, None),
        P(GZ, GY, None),
        P(GZ, GY, None),
        P(GZ, GY, None),
        P(GZ, GY, None),
        P(),
        P(),
        P(),
        P(),
    )
    return jax.shard_map(
        per_device,
        mesh=finer,
        in_specs=placed,
        out_specs=(P(GZ, GY, None), P(GZ, GY, None), P()),
        check_vma=False,
    )
```

profile of v0, /device:TPU:1, one launch (start us, length us, event | category | flops | bytes accessed | tf_op | source)
XLA Modules:
  0.0 252.9 jit_solution(12633689054472368846)
XLA Ops:
  0.6 1.0 fusion.81
  1.6 4.4 %collective-permute-start.6 = (f32[8,1,512]{2,1,0:T(1,128)S(1)}, f32[8,1,512]{2,1,0:T(1,128)S(1)}, u32[]{:S(2)}, u32[]{:S(2)}) collective-permute-start(f32[8,1,512]{2,1,0:T(1,128)S(1)} %get-tuple-element.47), channel_id=1, source_target_pairs={{0,1},{1,2},{2,3},{3,4},{4,5},{5,6},{6,7},{7,8},{8,9},{9,10},{10,1... | collective-permute-start | bytes 49160 | tf_op jit(solution)/shard_map/ppermute | solution.py:46
  6.0 1.3 collective-permute-start.7
  7.3 0.9 fusion.83
  8.2 2.9 %collective-permute-start.5 = (f32[1,32,512]{2,1,0:T(8,128)S(1)}, f32[1,32,512]{2,1,0:T(8,128)S(1)}, u32[]{:S(2)}, u32[]{:S(2)}) collective-permute-start(f32[1,32,512]{2,1,0:T(8,128)S(1)} %get-tuple-element.51), channel_id=1, source_target_pairs={{32,0},{64,32},{96,64},{128,96},{160,128},{192,160},{224,192},{33,... | collective-permute-start | bytes 196616 | tf_op jit(solution)/shard_map/ppermute | solution.py:47
  11.1 3.0 %collective-permute-start.4 = (f32[1,32,512]{2,1,0:T(8,128)S(1)}, f32[1,32,512]{2,1,0:T(8,128)S(1)}, u32[]{:S(2)}, u32[]{:S(2)}) collective-permute-start(f32[1,32,512]{2,1,0:T(8,128)S(1)} %get-tuple-element.52), channel_id=1, source_target_pairs={{0,32},{32,64},{64,96},{96,128},{128,160},{160,192},{192,224},{1,3... | collective-permute-start | bytes 196616 | tf_op jit(solution)/shard_map/ppermute | solution.py:46
  14.1 0.7 fusion.90
  14.8 6.8 %select_select_fusion = (f32[8,32,512]{2,1,0:T(8,128)S(1)}, pred[8,32,512]{2,1,0:T(8,128)(4,1)S(1)}, pred[8,32,512]{2,1,0:T(8,128)(4,1)S(1)}, pred[8,32,512]{2,1...) fusion(f32[]{:T(128)} %bitcast.31, f32[]{:T(128)} %bitcast.30, ...), kind=kLoop, calls=%fused_computation.135 | loop fusion | flops 2097152 | bytes 2097184 | tf_op jit(solution)/shard_map/jit(_where)/select_n | solution.py:61
  21.7 4.4 %collective-permute-start.2 = (f32[8,1,512]{2,1,0:T(1,128)S(1)}, f32[8,1,512]{2,1,0:T(1,128)S(1)}, u32[]{:S(2)}, u32[]{:S(2)}) collective-permute-start(f32[8,1,512]{2,1,0:T(1,128)S(1)} %get-tuple-element.45), channel_id=1, source_target_pairs={{0,1},{1,2},{2,3},{3,4},{4,5},{5,6},{6,7},{7,8},{8,9},{9,10},{10,1... | collective-permute-start | bytes 49160 | tf_op jit(solution)/shard_map/ppermute | solution.py:46
  26.1 0.7 fusion.87
  26.8 0.7 fusion.88
  27.5 0.7 fusion.89
  28.2 1.3 collective-permute-start.3
  29.6 2.8 %collective-permute-start = (f32[1,32,512]{2,1,0:T(8,128)S(1)}, f32[1,32,512]{2,1,0:T(8,128)S(1)}, u32[]{:S(2)}, u32[]{:S(2)}) collective-permute-start(f32[1,32,512]{2,1,0:T(8,128)S(1)} %get-tuple-element.49), channel_id=1, source_target_pairs={{0,32},{32,64},{64,96},{96,128},{128,160},{160,192},{192,224},{1,3... | collective-permute-start | bytes 196616 | tf_op jit(solution)/shard_map/ppermute | solution.py:46
  32.4 1.9 collective-permute-start.1
  34.4 3.6 %collective-permute-done.1 = f32[1,32,512]{2,1,0:T(8,128)S(1)} collective-permute-done((f32[1,32,512]{2,1,0:T(8,128)S(1)}, f32[1,32,512]{2,1,0:T(8,128)S(1)}, u32[]{:S(2)}, u32[]{:S(2)}) %collective-permute-start.1) | collective-permute-done | bytes 65568 | tf_op jit(solution)/shard_map/ppermute | solution.py:47
  38.1 18.1 %fusion.72 = (f32[8,32,512]{2,1,0:T(8,128)S(1)}, f32[8,32,512]{2,1,0:T(8,128)S(1)}, f32[8,32,512]{2,1,0:T(8,128)S(1)}, f32[8,32,512]{2,1,0:T(8,128)S(1)}, f32[8,32,512]{2,1,0:T(8,128)S(1)}) fusion(f32[8,32,512]{2,1,0:T(8,128)S(1)} %copy-done.2, f32[8,1,512]{2,1,0:T(1,128)S(1)} %collective-permute-done.7, ...), kind=kLoop, calls=%fused_computation.159 | loop fusion | flops 12582912 | bytes 7798880 | tf_op jit(solution)/shard_map/div | solution.py:128
  56.2 1.9 collective-permute-start.8
  58.1 2.4 collective-permute-start.9
  60.6 4.3 %collective-permute-start.10 = (f32[8,1,512]{2,1,0:T(1,128)S(1)}, f32[8,1,512]{2,1,0:T(1,128)S(1)}, u32[]{:S(2)}, u32[]{:S(2)}) collective-permute-start(f32[8,1,512]{2,1,0:T(1,128)S(1)} %get-tuple-element.41), channel_id=1, source_target_pairs={{0,1},{1,2},{2,3},{3,4},{4,5},{5,6},{6,7},{7,8},{8,9},{9,10},{10,1... | collective-permute-start | bytes 49160 | tf_op jit(solution)/shard_map/ppermute | solution.py:46
  64.9 1.3 collective-permute-start.11
  66.2 4.5 %collective-permute-done.11 = f32[8,1,512]{2,1,0:T(1,128)S(1)} collective-permute-done((f32[8,1,512]{2,1,0:T(1,128)S(1)}, f32[8,1,512]{2,1,0:T(1,128)S(1)}, u32[]{:S(2)}, u32[]{:S(2)}) %collective-permute-start.11) | collective-permute-done | bytes 16416 | tf_op jit(solution)/shard_map/ppermute | solution.py:47
  70.7 1.7 multiply_reduce_fusion.7
  72.4 1.3 pad_maximum_fusion.28
  73.8 21.9 %all_to_all.48 = f32[32,1,2]{2,1,0:T(1,128)} all-to-all(f32[32,1,2]{2,1,0:T(1,128)S(1)} %broadcast_in_dim.177), channel_id=1, replica_groups=mesh['gz_0'=4,'gz_1'=2,'gy_0'=4,'gy_1'=8] {'gy_0','gy_1'}, dimensions={0} | all-to-all | bytes 512 | tf_op jit(solution)/shard_map/all_to_all | solution.py:14
  95.6 1.3 reduce_sum.146
  96.9 0.7 broadcast_in_dim.178
  97.6 11.2 %all_to_all.49 = f32[8,1,2]{2,1,0:T(1,128)} all-to-all(f32[8,1,2]{2,1,0:T(1,128)S(1)} %broadcast_in_dim.178), channel_id=1, replica_groups=mesh['gz_0'=4,'gz_1'=2,'gy_0'=4,'gy_1'=8] {'gz_0','gz_1'}, dimensions={0} | all-to-all | bytes 128 | tf_op jit(solution)/shard_map/all_to_all | solution.py:14
  108.7 1.2 reduce_sum.147
  109.9 1.4 fusion.86
  112.7 1.2 fusion.70
  114.0 3.1 %collective-permute-start.12 = (f32[1,32,512]{2,1,0:T(8,128)S(1)}, f32[1,32,512]{2,1,0:T(8,128)S(1)}, u32[]{:S(2)}, u32[]{:S(2)}) collective-permute-start(f32[1,32,512]{2,1,0:T(8,128)S(1)} %get-tuple-element.39), channel_id=1, source_target_pairs={{0,32},{32,64},{64,96},{96,128},{128,160},{160,192},{192,224},{1,3... | collective-permute-start | bytes 196616 | tf_op jit(solution)/shard_map/ppermute | solution.py:46
  117.1 1.9 collective-permute-start.13
  119.0 2.3 collective-permute-start.14
  121.3 1.3 collective-permute-start.15
  122.6 3.2 %collective-permute-done.15 = f32[8,1,512]{2,1,0:T(1,128)S(1)} collective-permute-done((f32[8,1,512]{2,1,0:T(1,128)S(1)}, f32[8,1,512]{2,1,0:T(1,128)S(1)}, u32[]{:S(2)}, u32[]{:S(2)}) %collective-permute-start.15) | collective-permute-done | bytes 16416 | tf_op jit(solution)/shard_map/ppermute | solution.py:47
  125.8 2.5 multiply_reduce_fusion.5
  128.3 1.2 pad_maximum_fusion.29
  129.6 16.3 %all_to_all.50 = f32[32,1,2]{2,1,0:T(1,128)} all-to-all(f32[32,1,2]{2,1,0:T(1,128)S(1)} %broadcast_in_dim.179), channel_id=1, replica_groups=mesh['gz_0'=4,'gz_1'=2,'gy_0'=4,'gy_1'=8] {'gy_0','gy_1'}, dimensions={0} | all-to-all | bytes 512 | tf_op jit(solution)/shard_map/all_to_all | solution.py:14
  145.9 1.2 reduce_sum.150
  147.1 0.6 broadcast_in_dim.180
  147.7 11.1 %all_to_all.51 = f32[8,1,2]{2,1,0:T(1,128)} all-to-all(f32[8,1,2]{2,1,0:T(1,128)S(1)} %broadcast_in_dim.180), channel_id=1, replica_groups=mesh['gz_0'=4,'gz_1'=2,'gy_0'=4,'gy_1'=8] {'gz_0','gz_1'}, dimensions={0} | all-to-all | bytes 128 | tf_op jit(solution)/shard_map/all_to_all | solution.py:14
  158.7 1.2 reduce_sum.151
  159.9 1.3 fusion.85
  165.7 1.4 fusion.68
  167.2 3.1 %collective-permute-start.16 = (f32[1,32,512]{2,1,0:T(8,128)S(1)}, f32[1,32,512]{2,1,0:T(8,128)S(1)}, u32[]{:S(2)}, u32[]{:S(2)}) collective-permute-start(f32[1,32,512]{2,1,0:T(8,128)S(1)} %get-tuple-element.35), channel_id=1, source_target_pairs={{0,32},{32,64},{64,96},{96,128},{128,160},{160,192},{192,224},{1,3... | collective-permute-start | bytes 196616 | tf_op jit(solution)/shard_map/ppermute | solution.py:46
  170.2 1.9 collective-permute-start.17
  172.2 2.3 collective-permute-start.18
  174.5 1.3 collective-permute-start.19
  175.8 3.2 %collective-permute-done.19 = f32[8,1,512]{2,1,0:T(1,128)S(1)} collective-permute-done((f32[8,1,512]{2,1,0:T(1,128)S(1)}, f32[8,1,512]{2,1,0:T(1,128)S(1)}, u32[]{:S(2)}, u32[]{:S(2)}) %collective-permute-start.19) | collective-permute-done | bytes 16416 | tf_op jit(solution)/shard_map/ppermute | solution.py:47
  179.0 2.4 multiply_reduce_fusion.3
  181.4 1.2 pad_maximum_fusion.30
  182.6 16.2 %all_to_all.52 = f32[32,1,2]{2,1,0:T(1,128)S(1)} all-to-all(f32[32,1,2]{2,1,0:T(1,128)S(1)} %broadcast_in_dim.181), channel_id=1, replica_groups=mesh['gz_0'=4,'gz_1'=2,'gy_0'=4,'gy_1'=8] {'gy_0','gy_1'}, dimensions={0} | all-to-all | bytes 512 | tf_op jit(solution)/shard_map/all_to_all | solution.py:14
  198.8 11.3 %all_to_all.53 = f32[8,1,2]{2,1,0:T(1,128)S(1)} all-to-all(f32[8,1,2]{2,1,0:T(1,128)S(1)} %broadcast_in_dim.182), channel_id=1, replica_groups=mesh['gz_0'=4,'gz_1'=2,'gy_0'=4,'gy_1'=8] {'gz_0','gz_1'}, dimensions={0} | all-to-all | bytes 128 | tf_op jit(solution)/shard_map/all_to_all | solution.py:14
  210.1 0.6 fusion.84
  214.1 14.1 %multiply_reduce_fusion = (f32[]{:T(128)}, f32[8,32,512]{2,1,0:T(8,128)S(1)}, f32[8,32,512]{2,1,0:T(8,128)}) fusion(f32[8,32,512]{2,1,0:T(8,128)} %param.13, pred[8,32,512]{2,1,0:T(8,128)(4,1)} %copy-done.17, pred[8,32,512]{2,1,0:T(8,128)(4,1)} %copy-done.16, pred[8,32,512]{2,1,0:T(8,128)(4,1)} %copy-done.15, pred[8,32,512]{2,1,0:T(8,128)(4,1)} %copy-done.14, ...), kind=kLoop, calls=%fused_computation.117 | loop fusion | flops 4063231 | bytes 4194392 | tf_op jit(solution)/shard_map/reduce_sum | solution.py:149
  228.3 0.8 multiply_reduce_fusion.1
  229.1 1.3 pad_maximum_fusion.31
  230.4 11.6 %all_to_all.54 = f32[32,1,2]{2,1,0:T(1,128)S(1)} all-to-all(f32[32,1,2]{2,1,0:T(1,128)S(1)} %broadcast_in_dim.183), channel_id=1, replica_groups=mesh['gz_0'=4,'gz_1'=2,'gy_0'=4,'gy_1'=8] {'gy_0','gy_1'}, dimensions={0} | all-to-all | bytes 512 | tf_op jit(solution)/shard_map/all_to_all | solution.py:14
  242.1 0.6 broadcast_in_dim.184
  242.7 5.0 %all-to-all-start.7 = ((f32[8,1,2]{2,1,0:T(1,128)}), f32[8,1,2]{2,1,0:T(1,128)S(1)}, u32[]{:S(2)}, u32[]{:S(2)}) async-start(f32[8,1,2]{2,1,0:T(1,128)} %broadcast_in_dim.184), calls=%async_computation.7 | async-start | bytes 8192 | tf_op jit(solution)/shard_map/all_to_all | solution.py:14
  247.7 0.9 add.200
  248.6 3.7 %all-to-all-done.7 = f32[8,1,2]{2,1,0:T(1,128)S(1)} async-done(((f32[8,1,2]{2,1,0:T(1,128)}), f32[8,1,2]{2,1,0:T(1,128)S(1)}, u32[]{:S(2)}, u32[]{:S(2)}) %all-to-all-start.7) | async-done | bytes 96 | tf_op jit(solution)/shard_map/all_to_all | solution.py:14
  252.3 0.5 multiply_sqrt_fusion
  (102 shorter events, 0.6 us)
Async XLA Ops:
  1.6 28.0 %collective-permute-start.6 = (f32[8,1,512]{2,1,0:T(1,128)S(1)}, f32[8,1,512]{2,1,0:T(1,128)S(1)}, u32[]{:S(2)}, u32[]{:S(2)}) collective-permute-start(f32[8,1,512]{2,1,0:T(1,128)S(1)} %get-tuple-element.47), channel_id=1, source_target_pairs={{0,1},{1,2},{2,3},{3,4},{4,5},{5,6},{6,7},{7,8},{8,9},{9,10},{10,1... | collective-permute-start | bytes 49160 | tf_op jit(solution)/shard_map/ppermute | solution.py:46
  6.0 28.4 %collective-permute-start.7 = (f32[8,1,512]{2,1,0:T(1,128)S(1)}, f32[8,1,512]{2,1,0:T(1,128)S(1)}, u32[]{:S(2)}, u32[]{:S(2)}) collective-permute-start(f32[8,1,512]{2,1,0:T(1,128)S(1)} %get-tuple-element.48), channel_id=1, source_target_pairs={{1,0},{2,1},{3,2},{4,3},{5,4},{6,5},{7,6},{8,7},{9,8},{10,9},{11,1... | collective-permute-start | bytes 49160 | tf_op jit(solution)/shard_map/ppermute | solution.py:47
  8.2 5.9 %copy-start.29 = (f32[8]{0:T(128)S(1)}, f32[8]{0:T(128)}, u32[]{:S(2)}) copy-start(f32[8]{0:T(128)} %param.16) | copy-start | bytes 100
  8.2 24.2 %collective-permute-start.5 = (f32[1,32,512]{2,1,0:T(8,128)S(1)}, f32[1,32,512]{2,1,0:T(8,128)S(1)}, u32[]{:S(2)}, u32[]{:S(2)}) collective-permute-start(f32[1,32,512]{2,1,0:T(8,128)S(1)} %get-tuple-element.51), channel_id=1, source_target_pairs={{32,0},{64,32},{96,64},{128,96},{160,128},{192,160},{224,192},{33,... | collective-permute-start | bytes 196616 | tf_op jit(solution)/shard_map/ppermute | solution.py:47
  11.1 17.1 %collective-permute-start.4 = (f32[1,32,512]{2,1,0:T(8,128)S(1)}, f32[1,32,512]{2,1,0:T(8,128)S(1)}, u32[]{:S(2)}, u32[]{:S(2)}) collective-permute-start(f32[1,32,512]{2,1,0:T(8,128)S(1)} %get-tuple-element.52), channel_id=1, source_target_pairs={{0,32},{32,64},{64,96},{96,128},{128,160},{160,192},{192,224},{1,3... | collective-permute-start | bytes 196616 | tf_op jit(solution)/shard_map/ppermute | solution.py:46
  14.8 14.7 %copy-start.2 = (f32[8,32,512]{2,1,0:T(8,128)S(1)}, f32[8,32,512]{2,1,0:T(8,128)}, u32[]{:S(2)}) copy-start(f32[8,32,512]{2,1,0:T(8,128)} %param.13) | copy-start | bytes 1572868
  14.8 23.3 %copy-start.25 = (f32[8,32,512]{2,1,0:T(8,128)S(1)}, f32[8,32,512]{2,1,0:T(8,128)}, u32[]{:S(2)}) copy-start(f32[8,32,512]{2,1,0:T(8,128)} %param.12) | copy-start | bytes 1572868
  21.6 16.4 %copy-start.13 = (pred[8,32,512]{2,1,0:T(8,128)(4,1)}, pred[8,32,512]{2,1,0:T(8,128)(4,1)S(1)}, u32[]{:S(2)}) copy-start(pred[8,32,512]{2,1,0:T(8,128)(4,1)S(1)} %get-tuple-element.28) | copy-start | bytes 393220
  21.6 16.4 %copy-start.14 = (pred[8,32,512]{2,1,0:T(8,128)(4,1)}, pred[8,32,512]{2,1,0:T(8,128)(4,1)S(1)}, u32[]{:S(2)}) copy-start(pred[8,32,512]{2,1,0:T(8,128)(4,1)S(1)} %get-tuple-element.29) | copy-start | bytes 393220
  21.6 16.4 %copy-start.15 = (pred[8,32,512]{2,1,0:T(8,128)(4,1)}, pred[8,32,512]{2,1,0:T(8,128)(4,1)S(1)}, u32[]{:S(2)}) copy-start(pred[8,32,512]{2,1,0:T(8,128)(4,1)S(1)} %get-tuple-element.30) | copy-start | bytes 393220
  21.6 16.4 %copy-start.16 = (pred[8,32,512]{2,1,0:T(8,128)(4,1)}, pred[8,32,512]{2,1,0:T(8,128)(4,1)S(1)}, u32[]{:S(2)}) copy-start(pred[8,32,512]{2,1,0:T(8,128)(4,1)S(1)} %get-tuple-element.31) | copy-start | bytes 393220
  21.6 16.4 %copy-start.17 = (pred[8,32,512]{2,1,0:T(8,128)(4,1)}, pred[8,32,512]{2,1,0:T(8,128)(4,1)S(1)}, u32[]{:S(2)}) copy-start(pred[8,32,512]{2,1,0:T(8,128)(4,1)S(1)} %get-tuple-element.32) | copy-start | bytes 393220
  21.6 4.5 %copy-start.30 = (f32[8]{0:T(128)S(1)}, f32[8]{0:T(128)}, u32[]{:S(2)}) copy-start(f32[8]{0:T(128)} %param.17) | copy-start | bytes 100
  21.6 5.2 %copy-start.31 = (f32[8]{0:T(128)S(1)}, f32[8]{0:T(128)}, u32[]{:S(2)}) copy-start(f32[8]{0:T(128)} %param.18) | copy-start | bytes 100
  21.6 5.9 %copy-start.32 = (f32[8]{0:T(128)S(1)}, f32[8]{0:T(128)}, u32[]{:S(2)}) copy-start(f32[8]{0:T(128)} %param.19) | copy-start | bytes 100
  21.7 12.7 %collective-permute-start.2 = (f32[8,1,512]{2,1,0:T(1,128)S(1)}, f32[8,1,512]{2,1,0:T(1,128)S(1)}, u32[]{:S(2)}, u32[]{:S(2)}) collective-permute-start(f32[8,1,512]{2,1,0:T(1,128)S(1)} %get-tuple-element.45), channel_id=1, source_target_pairs={{0,1},{1,2},{2,3},{3,4},{4,5},{5,6},{6,7},{7,8},{8,9},{9,10},{10,1... | collective-permute-start | bytes 49160 | tf_op jit(solution)/shard_map/ppermute | solution.py:46
  26.1 12.0 %copy-start.24 = (f32[8,32,512]{2,1,0:T(8,128)S(1)}, f32[8,32,512]{2,1,0:T(8,128)}, u32[]{:S(2)}) copy-start(f32[8,32,512]{2,1,0:T(8,128)} %param.15) | copy-start | bytes 1572868
  28.2 6.2 %collective-permute-start.3 = (f32[8,1,512]{2,1,0:T(1,128)S(1)}, f32[8,1,512]{2,1,0:T(1,128)S(1)}, u32[]{:S(2)}, u32[]{:S(2)}) collective-permute-start(f32[8,1,512]{2,1,0:T(1,128)S(1)} %get-tuple-element.46), channel_id=1, source_target_pairs={{1,0},{2,1},{3,2},{4,3},{5,4},{6,5},{7,6},{8,7},{9,8},{10,9},{11,1... | collective-permute-start | bytes 49160 | tf_op jit(solution)/shard_map/ppermute | solution.py:47
  29.5 8.6 %copy-start = (s32[8,32,512]{2,1,0:T(8,128)S(1)}, s32[8,32,512]{2,1,0:T(8,128)}, u32[]{:S(2)}) copy-start(s32[8,32,512]{2,1,0:T(8,128)} %param.11) | copy-start | bytes 1572868
  29.5 8.6 %copy-start.10 = (f32[8,32,512]{2,1,0:T(8,128)S(1)}, f32[8,32,512]{2,1,0:T(8,128)}, u32[]{:S(2)}) copy-start(f32[8,32,512]{2,1,0:T(8,128)} %param.14) | copy-start | bytes 1572868
  29.6 4.8 %collective-permute-start = (f32[1,32,512]{2,1,0:T(8,128)S(1)}, f32[1,32,512]{2,1,0:T(8,128)S(1)}, u32[]{:S(2)}, u32[]{:S(2)}) collective-permute-start(f32[1,32,512]{2,1,0:T(8,128)S(1)} %get-tuple-element.49), channel_id=1, source_target_pairs={{0,32},{32,64},{64,96},{96,128},{128,160},{160,192},{192,224},{1,3... | collective-permute-start | bytes 196616 | tf_op jit(solution)/shard_map/ppermute | solution.py:46
  32.4 5.6 %collective-permute-start.1 = (f32[1,32,512]{2,1,0:T(8,128)S(1)}, f32[1,32,512]{2,1,0:T(8,128)S(1)}, u32[]{:S(2)}, u32[]{:S(2)}) collective-permute-start(f32[1,32,512]{2,1,0:T(8,128)S(1)} %get-tuple-element.50), channel_id=1, source_target_pairs={{32,0},{64,32},{96,64},{128,96},{160,128},{192,160},{224,192},{33,... | collective-permute-start | bytes 196616 | tf_op jit(solution)/shard_map/ppermute | solution.py:47
  34.4 36.3 %copy-start.26 = (f32[8,1,512]{2,1,0:T(1,128)}, f32[8,1,512]{2,1,0:T(1,128)S(1)}, u32[]{:S(2)}) copy-start(f32[8,1,512]{2,1,0:T(1,128)S(1)} %collective-permute-done.3) | copy-start | bytes 49156
  34.4 36.3 %copy-start.18 = (f32[1,32,512]{2,1,0:T(8,128)}, f32[1,32,512]{2,1,0:T(8,128)S(1)}, u32[]{:S(2)}) copy-start(f32[1,32,512]{2,1,0:T(8,128)S(1)} %collective-permute-done) | copy-start | bytes 196612
  38.0 32.7 %copy-start.21 = (f32[1,32,512]{2,1,0:T(8,128)}, f32[1,32,512]{2,1,0:T(8,128)S(1)}, u32[]{:S(2)}) copy-start(f32[1,32,512]{2,1,0:T(8,128)S(1)} %collective-permute-done.1) | copy-start | bytes 196612
  56.2 16.2 %copy-start.1 = (f32[8,32,512]{2,1,0:T(8,128)}, f32[8,32,512]{2,1,0:T(8,128)S(1)}, u32[]{:S(2)}) copy-start(f32[8,32,512]{2,1,0:T(8,128)S(1)} %get-tuple-element.19) | copy-start | bytes 1572868
  56.2 16.2 %copy-start.8 = (f32[8,32,512]{2,1,0:T(8,128)}, f32[8,32,512]{2,1,0:T(8,128)S(1)}, u32[]{:S(2)}) copy-start(f32[8,32,512]{2,1,0:T(8,128)S(1)} %get-tuple-element.20) | copy-start | bytes 1572868
  56.2 14.5 %collective-permute-start.8 = (f32[1,32,512]{2,1,0:T(8,128)S(1)}, f32[1,32,512]{2,1,0:T(8,128)S(1)}, u32[]{:S(2)}, u32[]{:S(2)}) collective-permute-start(f32[1,32,512]{2,1,0:T(8,128)S(1)} %get-tuple-element.43), channel_id=1, source_target_pairs={{0,32},{32,64},{64,96},{96,128},{128,160},{160,192},{192,224},{1,3... | collective-permute-start | bytes 196616 | tf_op jit(solution)/shard_map/ppermute | solution.py:46
  58.1 12.6 %collective-permute-start.9 = (f32[1,32,512]{2,1,0:T(8,128)S(1)}, f32[1,32,512]{2,1,0:T(8,128)S(1)}, u32[]{:S(2)}, u32[]{:S(2)}) collective-permute-start(f32[1,32,512]{2,1,0:T(8,128)S(1)} %get-tuple-element.44), channel_id=1, source_target_pairs={{32,0},{64,32},{96,64},{128,96},{160,128},{192,160},{224,192},{33,... | collective-permute-start | bytes 196616 | tf_op jit(solution)/shard_map/ppermute | solution.py:47
  60.6 5.6 %collective-permute-start.10 = (f32[8,1,512]{2,1,0:T(1,128)S(1)}, f32[8,1,512]{2,1,0:T(1,128)S(1)}, u32[]{:S(2)}, u32[]{:S(2)}) collective-permute-start(f32[8,1,512]{2,1,0:T(1,128)S(1)} %get-tuple-element.41), channel_id=1, source_target_pairs={{0,1},{1,2},{2,3},{3,4},{4,5},{5,6},{6,7},{7,8},{8,9},{9,10},{10,1... | collective-permute-start | bytes 49160 | tf_op jit(solution)/shard_map/ppermute | solution.py:46
  64.9 5.9 %collective-permute-start.11 = (f32[8,1,512]{2,1,0:T(1,128)S(1)}, f32[8,1,512]{2,1,0:T(1,128)S(1)}, u32[]{:S(2)}, u32[]{:S(2)}) collective-permute-start(f32[8,1,512]{2,1,0:T(1,128)S(1)} %get-tuple-element.42), channel_id=1, source_target_pairs={{1,0},{2,1},{3,2},{4,3},{5,4},{6,5},{7,6},{8,7},{9,8},{10,9},{11,1... | collective-permute-start | bytes 49160 | tf_op jit(solution)/shard_map/ppermute | solution.py:47
  113.9 14.4 %copy-start.3 = (f32[8,32,512]{2,1,0:T(8,128)}, f32[8,32,512]{2,1,0:T(8,128)S(1)}, u32[]{:S(2)}) copy-start(f32[8,32,512]{2,1,0:T(8,128)S(1)} %get-tuple-element.16) | copy-start | bytes 1572868
  113.9 14.4 %copy-start.9 = (f32[8,32,512]{2,1,0:T(8,128)}, f32[8,32,512]{2,1,0:T(8,128)S(1)}, u32[]{:S(2)}) copy-start(f32[8,32,512]{2,1,0:T(8,128)S(1)} %get-tuple-element.17) | copy-start | bytes 1572868
  114.0 11.8 %copy-start.22 = (f32[1,32,512]{2,1,0:T(8,128)S(1)}, f32[1,32,512]{2,1,0:T(8,128)}, u32[]{:S(2)}) copy-start(f32[1,32,512]{2,1,0:T(8,128)} %copy-done.21) | copy-start | bytes 196612
  114.0 11.8 %copy-start.27 = (f32[8,1,512]{2,1,0:T(1,128)S(1)}, f32[8,1,512]{2,1,0:T(1,128)}, u32[]{:S(2)}) copy-start(f32[8,1,512]{2,1,0:T(1,128)} %copy-done.26) | copy-start | bytes 49156
  114.0 11.8 %copy-start.19 = (f32[1,32,512]{2,1,0:T(8,128)S(1)}, f32[1,32,512]{2,1,0:T(8,128)}, u32[]{:S(2)}) copy-start(f32[1,32,512]{2,1,0:T(8,128)} %copy-done.18) | copy-start | bytes 196612
  114.0 11.8 %collective-permute-start.12 = (f32[1,32,512]{2,1,0:T(8,128)S(1)}, f32[1,32,512]{2,1,0:T(8,128)S(1)}, u32[]{:S(2)}, u32[]{:S(2)}) collective-permute-start(f32[1,32,512]{2,1,0:T(8,128)S(1)} %get-tuple-element.39), channel_id=1, source_target_pairs={{0,32},{32,64},{64,96},{96,128},{128,160},{160,192},{192,224},{1,3... | collective-permute-start | bytes 196616 | tf_op jit(solution)/shard_map/ppermute | solution.py:46
  117.1 8.7 %collective-permute-start.13 = (f32[1,32,512]{2,1,0:T(8,128)S(1)}, f32[1,32,512]{2,1,0:T(8,128)S(1)}, u32[]{:S(2)}, u32[]{:S(2)}) collective-permute-start(f32[1,32,512]{2,1,0:T(8,128)S(1)} %get-tuple-element.40), channel_id=1, source_target_pairs={{32,0},{64,32},{96,64},{128,96},{160,128},{192,160},{224,192},{33,... | collective-permute-start | bytes 196616 | tf_op jit(solution)/shard_map/ppermute | solution.py:47
  119.0 3.6 %collective-permute-start.14 = (f32[8,1,512]{2,1,0:T(1,128)S(1)}, f32[8,1,512]{2,1,0:T(1,128)S(1)}, u32[]{:S(2)}, u32[]{:S(2)}) collective-permute-start(f32[8,1,512]{2,1,0:T(1,128)S(1)} %get-tuple-element.37), channel_id=1, source_target_pairs={{0,1},{1,2},{2,3},{3,4},{4,5},{5,6},{6,7},{7,8},{8,9},{9,10},{10,1... | collective-permute-start | bytes 49160 | tf_op jit(solution)/shard_map/ppermute | solution.py:46
  121.3 4.5 %collective-permute-start.15 = (f32[8,1,512]{2,1,0:T(1,128)S(1)}, f32[8,1,512]{2,1,0:T(1,128)S(1)}, u32[]{:S(2)}, u32[]{:S(2)}) collective-permute-start(f32[8,1,512]{2,1,0:T(1,128)S(1)} %get-tuple-element.38), channel_id=1, source_target_pairs={{1,0},{2,1},{3,2},{4,3},{5,4},{6,5},{7,6},{8,7},{9,8},{10,9},{11,1... | collective-permute-start | bytes 49160 | tf_op jit(solution)/shard_map/ppermute | solution.py:47
  167.1 14.3 %copy-start.4 = (f32[8,32,512]{2,1,0:T(8,128)}, f32[8,32,512]{2,1,0:T(8,128)S(1)}, u32[]{:S(2)}) copy-start(f32[8,32,512]{2,1,0:T(8,128)S(1)} %get-tuple-element.13) | copy-start | bytes 1572868
  167.1 14.3 %copy-start.6 = (f32[8,32,512]{2,1,0:T(8,128)}, f32[8,32,512]{2,1,0:T(8,128)S(1)}, u32[]{:S(2)}) copy-start(f32[8,32,512]{2,1,0:T(8,128)S(1)} %get-tuple-element.14) | copy-start | bytes 1572868
  167.1 11.8 %copy-start.23 = (f32[1,32,512]{2,1,0:T(8,128)S(1)}, f32[1,32,512]{2,1,0:T(8,128)}, u32[]{:S(2)}) copy-start(f32[1,32,512]{2,1,0:T(8,128)} %copy-done.21) | copy-start | bytes 196612
  167.1 11.8 %copy-start.28 = (f32[8,1,512]{2,1,0:T(1,128)S(1)}, f32[8,1,512]{2,1,0:T(1,128)}, u32[]{:S(2)}) copy-start(f32[8,1,512]{2,1,0:T(1,128)} %copy-done.26) | copy-start | bytes 49156
  167.2 11.8 %copy-start.20 = (f32[1,32,512]{2,1,0:T(8,128)S(1)}, f32[1,32,512]{2,1,0:T(8,128)}, u32[]{:S(2)}) copy-start(f32[1,32,512]{2,1,0:T(8,128)} %copy-done.18) | copy-start | bytes 196612
  167.2 11.8 %collective-permute-start.16 = (f32[1,32,512]{2,1,0:T(8,128)S(1)}, f32[1,32,512]{2,1,0:T(8,128)S(1)}, u32[]{:S(2)}, u32[]{:S(2)}) collective-permute-start(f32[1,32,512]{2,1,0:T(8,128)S(1)} %get-tuple-element.35), channel_id=1, source_target_pairs={{0,32},{32,64},{64,96},{96,128},{128,160},{160,192},{192,224},{1,3... | collective-permute-start | bytes 196616 | tf_op jit(solution)/shard_map/ppermute | solution.py:46
  170.2 8.7 %collective-permute-start.17 = (f32[1,32,512]{2,1,0:T(8,128)S(1)}, f32[1,32,512]{2,1,0:T(8,128)S(1)}, u32[]{:S(2)}, u32[]{:S(2)}) collective-permute-start(f32[1,32,512]{2,1,0:T(8,128)S(1)} %get-tuple-element.36), channel_id=1, source_target_pairs={{32,0},{64,32},{96,64},{128,96},{160,128},{192,160},{224,192},{33,... | collective-permute-start | bytes 196616 | tf_op jit(solution)/shard_map/ppermute | solution.py:47
  172.2 3.6 %collective-permute-start.18 = (f32[8,1,512]{2,1,0:T(1,128)S(1)}, f32[8,1,512]{2,1,0:T(1,128)S(1)}, u32[]{:S(2)}, u32[]{:S(2)}) collective-permute-start(f32[8,1,512]{2,1,0:T(1,128)S(1)} %get-tuple-element.33), channel_id=1, source_target_pairs={{0,1},{1,2},{2,3},{3,4},{4,5},{5,6},{6,7},{7,8},{8,9},{9,10},{10,1... | collective-permute-start | bytes 49160 | tf_op jit(solution)/shard_map/ppermute | solution.py:46
  174.5 4.5 %collective-permute-start.19 = (f32[8,1,512]{2,1,0:T(1,128)S(1)}, f32[8,1,512]{2,1,0:T(1,128)S(1)}, u32[]{:S(2)}, u32[]{:S(2)}) collective-permute-start(f32[8,1,512]{2,1,0:T(1,128)S(1)} %get-tuple-element.34), channel_id=1, source_target_pairs={{1,0},{2,1},{3,2},{4,3},{5,4},{6,5},{7,6},{8,7},{9,8},{10,9},{11,1... | collective-permute-start | bytes 49160 | tf_op jit(solution)/shard_map/ppermute | solution.py:47
  214.1 14.2 %copy-start.5 = (f32[8,32,512]{2,1,0:T(8,128)S(1)}, f32[8,32,512]{2,1,0:T(8,128)}, u32[]{:S(2)}) copy-start(f32[8,32,512]{2,1,0:T(8,128)} %get-tuple-element.15) | copy-start | bytes 1572868
  214.1 14.2 %copy-start.7 = (f32[8,32,512]{2,1,0:T(8,128)S(1)}, f32[8,32,512]{2,1,0:T(8,128)}, u32[]{:S(2)}) copy-start(f32[8,32,512]{2,1,0:T(8,128)} %copy-done.6) | copy-start | bytes 1572868
  214.1 14.2 %copy-start.12 = (f32[8,32,512]{2,1,0:T(8,128)S(1)}, f32[8,32,512]{2,1,0:T(8,128)}, u32[]{:S(2)}) copy-start(f32[8,32,512]{2,1,0:T(8,128)} %get-tuple-element.12) | copy-start | bytes 1572868
  228.3 19.4 %copy-start.11 = (f32[8,32,512]{2,1,0:T(8,128)S(1)}, f32[8,32,512]{2,1,0:T(8,128)}, u32[]{:S(2)}) copy-start(f32[8,32,512]{2,1,0:T(8,128)} %param.14) | copy-start | bytes 1572868
  242.7 9.6 %all-to-all-start.7 = ((f32[8,1,2]{2,1,0:T(1,128)}), f32[8,1,2]{2,1,0:T(1,128)S(1)}, u32[]{:S(2)}, u32[]{:S(2)}) async-start(f32[8,1,2]{2,1,0:T(1,128)} %broadcast_in_dim.184), calls=%async_computation.7 | async-start | bytes 8192 | tf_op jit(solution)/shard_map/all_to_all | solution.py:14
where the time goes:
time: 255 us; the launch traced here: 253 us
  blocking collectives  99.5 us (39%)
  other arithmetic  60.5 us (24%)
  starting transfers between devices  53.9 us (21%)
  waiting for transfers between devices  18.3 us (7%)
  between operations  10.6 us (4%)
  local copies, waits for them, and re-layouts  10.1 us (4%)
    all_to_all x7, blocking collectives, copy_for_each(): lax.all_to_all(jnp.broadcast_to(array[None], (size, *array.shape)), axis,...  99.5 us
    ppermute x10, starting transfers between devices, with_halo(): lax.ppermute(last, axis, up)  31.4 us
    div x3, other arithmetic, per_device(): precond = residual / diagonal  20.7 us
    ppermute x10, starting transfers between devices, with_halo(): lax.ppermute(first, axis, [(b, a) for a, b in up])  17.5 us
    ppermute x10, waiting for transfers between devices, with_halo(): lax.ppermute(first, axis, [(b, a) for a, b in up])  14.5 us
    reduce_sum x1, other arithmetic, per_device(): jnp.sum(change * change)  14.1 us
    select_n x1, other arithmetic, lookup(): result = jnp.where(zone_ids == zone_index, zone_table[zone_index], result)  6.78 us
    reduce_sum x3, other arithmetic, paired_totals(): jnp.sum(residual * precond)  6.53 us
  transfers between devices with their start and end apart: 21, of which 5 were waited for; matrix products, arithmetic and copies ran while one was open for 5% of the time, Pallas kernels for 0%

commit v1 on v0

v1 whole, which is shorter than its diff:
```python
import jax
import jax.numpy as jnp
from jax import lax
from jax.experimental import pallas as pl
from jax.experimental.pallas import tpu as pltpu
from jax.sharding import PartitionSpec as P

MESH = pl.DeviceIdType.MESH
F32 = jnp.float32
CORES = 2
LINE = 8
LANES = 128
HALO = 3
TOP = 8
SUMS = 24


def halo_box(side_z, side_y, depth_z, depth_y, nz, ny):
    def one(side, depth, base, size):
        if side == 0:
            return base, base, size
        if side > 0:
            return base, base + size, depth
        return base + size - depth, base - depth, depth

    sz, dz, lz = one(side_z, depth_z, HALO, nz)
    sy, dy, ly = one(side_y, depth_y, TOP, ny)
    src = (pl.ds(sz, lz), slice(None), pl.ds(sy, ly))
    dst = (pl.ds(dz, lz), slice(None), pl.ds(dy, ly))
    return src, dst


FACES = ((-1, 0), (1, 0), (0, -1), (0, 1))
CORNERS = ((-1, -1), (-1, 1), (1, -1), (1, 1))


def pick(zone, table):
    b0 = (zone & 1) != 0
    b1 = (zone & 2) != 0
    b2 = (zone & 4) != 0

    def one(t):
        low = [jnp.where(b0, t[2 * i + 1], t[2 * i]) for i in range(4)]
        mid = [jnp.where(b1, low[2 * i + 1], low[2 * i]) for i in range(2)]
        return jnp.where(b2, mid[1], mid[0])

    return [one(t) for t in table]


def harmonic(a, b):
    return 2.0 * a * b / jnp.maximum(a + b, 1e-20)


def body(shape_z, shape_y, nz, ny, nt, zone_hbm, fixed_hbm, old_hbm, iter_hbm, strain_hbm,
         source_hbm, perm_s, stor_s, biot_s, bulk_s, press_out, strain_out, norms_out,
         zb, fb, pb, kb, fx, fy, fz, cb, u0, u1, u2, db, gb, bb, ob, sb, qb,
         partial, slots_a, mid, slots_b,
         lsem, ssem, rsem, asem, arsem, bsem, brsem):
    gz = lax.axis_index("gz")
    gy = lax.axis_index("gy")
    chips = shape_z // CORES
    rows_y = shape_y // LINE
    my_x, my_core = gz // CORES, gz % CORES
    my_y, my_z = gy // LINE, gy % LINE

    def near(side_z, side_y):
        return ((gz - side_z + shape_z) % shape_z, (gy - side_y + shape_y) % shape_y)

    size_a = LINE * CORES
    size_b = chips * rows_y
    rank_a = my_z * CORES + my_core
    rank_b = my_y * chips + my_x

    def peer_a(rank):
        return (my_x * CORES + rank % CORES, my_y * LINE + rank // CORES)

    def peer_b(rank):
        return (rank % chips * CORES + my_core, rank // chips * LINE + my_z)

    barrier = pltpu.get_barrier_semaphore()
    for j in range(1, size_a):
        pl.semaphore_signal(barrier, inc=1, device_id=peer_a((rank_a + j) % size_a), device_id_type=MESH)
    for j in range(1, size_b):
        pl.semaphore_signal(barrier, inc=1, device_id=peer_b((rank_b + j) % size_b), device_id_type=MESH)
    for side in FACES + CORNERS:
        pl.semaphore_signal(barrier, inc=1, device_id=near(*side), device_id_type=MESH)

    loads = []
    for n, (src, dst, ext) in enumerate((
        (zone_hbm, zb, True), (iter_hbm, pb, True), (fixed_hbm, fb, True),
        (old_hbm, ob, False), (strain_hbm, sb, False), (source_hbm, qb, False),
    )):
        group = []
        for t in range(nt):
            view = src.at[:, :, pl.ds(LANES * t, LANES)]
            if ext:
                into = dst.at[pl.ds(HALO, nz), t, pl.ds(TOP, ny), :]
            else:
                into = dst.at[:, t]
            copy = pltpu.make_async_copy(view, into, lsem.at[n, t])
            copy.start()
            group.append(copy)
        loads.append(group)

    for group in loads[:3]:
        for copy in group:
            copy.wait()
    pl.semaphore_wait(barrier, size_a - 1 + size_b - 1 + len(FACES) + len(CORNERS))

    counter = [0]

    def send(ref, side, depth_z, depth_y):
        src, dst = halo_box(side[0], side[1], depth_z, depth_y, nz, ny)
        i = counter[0]
        counter[0] += 1
        copy = pltpu.make_async_remote_copy(
            src_ref=ref.at[src], dst_ref=ref.at[dst], send_sem=ssem.at[i], recv_sem=rsem.at[i],
            device_id=near(*side), device_id_type=MESH)
        copy.start()
        return copy

    first = [send(pb, side, 1, 1) for side in FACES]
    first += [send(zb, side, 3, 3) for side in FACES]
    first += [send(zb, side, 2, 2) for side in CORNERS]
    later = [send(fb, side, 2, 2) for side in FACES]
    later += [send(fb, side, 1, 1) for side in CORNERS]

    for group in loads[3:]:
        for copy in group:
            copy.wait()

    perm = [perm_s[i] for i in range(8)]
    stor = [stor_s[i] for i in range(8)]
    biot = [biot_s[i] for i in range(8)]
    gain = [biot_s[i] / bulk_s[i] for i in range(8)]
    coup = [biot[i] * biot[i] / bulk_s[i] for i in range(8)]
    keep = [stor[i] + coup[i] for i in range(8)]

    lane = lax.broadcasted_iota(jnp.int32, (8, LANES), 1)
    own = pl.ds(TOP, ny)

    @pl.loop(0, nz)
    def _(z):
        for t in range(nt):
            s, a, c, g, k = pick(zb[z + HALO, t, own, :], (stor, biot, coup, gain, perm))
            kb[z + HALO, t, own, :] = k
            gb[z, t] = g
            db[z, t] = s + c
            bb[z, t] = s * ob[z, t] + c * pb[z + HALO, t, own, :] - a * sb[z, t] + qb[z, t]

    for copy in first:
        copy.wait()

    has_lo, has_hi = gz > 0, gz < shape_z - 1
    has_below, has_above = gy > 0, gy < shape_y - 1

    def put_perm(z, start, size, live):
        row = lax.broadcasted_iota(jnp.int32, (size, LANES), 0) + start
        inside = ((row >= TOP) | has_below) & ((row < TOP + ny) | has_above) & live
        for t in range(nt):
            (k,) = pick(zb[z, t, pl.ds(start, size), :], (perm,))
            kb[z, t, pl.ds(start, size), :] = jnp.where(inside, k, 0.0)

    for z in range(HALO):
        put_perm(z, 0, 48, has_lo)
        put_perm(z + HALO + nz, 0, 48, has_hi)

    @pl.loop(HALO, HALO + nz)
    def _(z):
        put_perm(z, 0, 8, gz >= 0)
        put_perm(z, TOP + ny, 8, gz >= 0)

    def x_up(tiles, wrap):
        rolled = [pltpu.roll(v, LANES - 1, 1) for v in tiles]
        last = lax.broadcasted_iota(jnp.int32, tiles[0].shape, 1) == LANES - 1
        out = []
        for t in range(nt):
            nxt = rolled[t + 1] if t + 1 < nt else (rolled[0] if wrap else jnp.zeros_like(rolled[0]))
            out.append(jnp.where(last, nxt, rolled[t]))
        return out

    def x_down(tiles):
        rolled = [pltpu.roll(v, 1, 1) for v in tiles]
        head = lax.broadcasted_iota(jnp.int32, tiles[0].shape, 1) == 0
        return [jnp.where(head, rolled[t - 1], rolled[t]) for t in range(nt)]

    def put_faces_x(z, start, size):
        rows = pl.ds(start, size)
        k = [kb[z, t, rows, :] for t in range(nt)]
        up = x_up(k, False)
        for t in range(nt):
            fx[z, t, rows, :] = harmonic(k[t], up[t])

    def put_faces_y(z, start, size):
        for t in range(nt):
            fy[z, t, pl.ds(start, size), :] = harmonic(
                kb[z, t, pl.ds(start, size), :], kb[z, t, pl.ds(start + 1, size), :])

    def put_faces_z(z, start, size):
        for t in range(nt):
            fz[z, t, pl.ds(start, size), :] = harmonic(
                kb[z, t, pl.ds(start, size), :], kb[z + 1, t, pl.ds(start, size), :])

    def diagonal(base, z, start, size):
        rows = pl.ds(start, size)
        low_x = x_down([fx[z, t, rows, :] for t in range(nt)])
        out = []
        for t in range(nt):
            d = base[t] + fz[z - 1, t, rows, :] + fz[z, t, rows, :]
            d = d + fy[z, t, pl.ds(start - 1, size), :] + fy[z, t, rows, :]
            out.append(d + low_x[t] + fx[z, t, rows, :])
        return out

    def around(src, z, start, size):
        rows, under, over = pl.ds(start, size), pl.ds(start - 1, size), pl.ds(start + 1, size)
        mid_v = [src[z, t, rows, :] for t in range(nt)]
        face = [fx[z, t, rows, :] for t in range(nt)]
        up = x_up(mid_v, True)
        down = x_down([face[t] * mid_v[t] for t in range(nt)])
        out = []
        for t in range(nt):
            total = fz[z - 1, t, rows, :] * src[z - 1, t, rows, :] + fz[z, t, rows, :] * src[z + 1, t, rows, :]
            total = total + fy[z, t, under, :] * src[z, t, under, :] + fy[z, t, rows, :] * src[z, t, over, :]
            out.append(total + down[t] + face[t] * up[t])
        return out

    put_faces_z(HALO - 1, TOP, ny)

    @pl.loop(HALO, HALO + nz)
    def _(z):
        put_faces_z(z, TOP, ny)
        put_faces_y(z, 7, 40)
        put_faces_x(z, TOP, ny)

    @pl.loop(0, nz)
    def _(z):
        zz = z + HALO
        diag = diagonal([db[z, t] for t in range(nt)], zz, TOP, ny)
        near_sum = around(pb, zz, TOP, ny)
        for t in range(nt):
            d = diag[t]
            free = 1.0 - fb[zz, t, own, :].astype(F32)
            c = free / d
            db[z, t] = d
            cb[zz, t, own, :] = c
            u0[zz, t, own, :] = c * (bb[z, t] - (d * pb[zz, t, own, :] - near_sum[t]))

    second = [send(u0, side, 3, 3) for side in FACES]
    second += [send(u0, side, 2, 2) for side in CORNERS]

    for copy in later:
        copy.wait()

    def put_scale(z, start, size):
        rows = pl.ds(start, size)
        base = [pick(zb[z, t, rows, :], (keep,))[0] for t in range(nt)]
        diag = diagonal(base, z, start, size)
        for t in range(nt):
            cb[z, t, rows, :] = (1.0 - fb[z, t, rows, :].astype(F32)) / diag[t]

    put_faces_z(0, 5, 40)
    for z in (1, 2, HALO + nz, HALO + nz + 1):
        put_faces_z(z, 5, 40)
        put_faces_y(z, 5, 40)
        put_faces_x(z, 5, 40)

    @pl.loop(HALO, HALO + nz)
    def _(z):
        for start in (0, 39):
            put_faces_z(z, start, 8)
            put_faces_y(z, start, 8)
            put_faces_x(z, start, 8)

    for z in (1, 2, HALO + nz, HALO + nz + 1):
        put_scale(z, 6, 40)

    @pl.loop(HALO, HALO + nz)
    def _(z):
        for start in (1, 39):
            put_scale(z, start, 8)

    for copy in second:
        copy.wait()

    @pl.loop(1, HALO + nz + 2)
    def _(z):
        new = around(u0, z, 6, 40)
        for t in range(nt):
            u1[z, t, pl.ds(6, 40), :] = cb[z, t, pl.ds(6, 40), :] * new[t]

    @pl.loop(2, HALO + nz + 1)
    def _(z):
        new = around(u1, z, 7, 40)
        for t in range(nt):
            u2[z, t, pl.ds(7, 40), :] = cb[z, t, pl.ds(7, 40), :] * new[t]

    def fold(v):
        total = v[0:8]
        for i in range(8, v.shape[0], 8):
            total = total + v[i:i + 8]
        return total

    def gram_step(z, acc):
        zz = z + HALO
        new = around(u2, zz, TOP, ny)
        acc = list(acc)
        for t in range(nt):
            d, g = db[z, t], gb[z, t]
            u = [u0[zz, t, own, :], u1[zz, t, own, :], u2[zz, t, own, :]]
            free = 1.0 - fb[zz, t, own, :].astype(F32)
            w = [d * v for v in u] + [free * new[t]]
            s = [g * v for v in u]
            e = 0
            for i, j in ((0, 0), (0, 1), (1, 1), (1, 2), (2, 2), (2, 3)):
                acc[e] = acc[e] + fold(u[i] * w[j])
                e += 1
            for i in range(4):
                for j in range(i, 4):
                    acc[e] = acc[e] + fold(w[i] * w[j])
                    e += 1
            for i in range(3):
                for j in range(i, 3):
                    acc[e] = acc[e] + fold(s[i] * s[j])
                    e += 1
        return tuple(acc)

    zero = jnp.zeros((8, LANES), F32)
    acc = list(lax.fori_loop(0, nz, gram_step, (zero,) * 22))
    acc += [zero] * (SUMS - len(acc))

    sub = lax.broadcasted_iota(jnp.int32, (8, LANES), 0)

    def merge(a, b, step):
        take = (sub & step) == 0
        return jnp.where(take, a, b) + pltpu.roll(jnp.where(take, b, a), step, 0)

    line = jnp.zeros((8, LANES), F32)
    for i in range(SUMS // 8):
        rows8 = acc[8 * i:8 * i + 8]
        four = [merge(rows8[j], rows8[j + 1], 1) for j in range(0, 8, 2)]
        two = [merge(four[j], four[j + 1], 2) for j in range(0, 4, 2)]
        one = merge(two[0], two[1], 4)
        whole = jnp.sum(one, axis=1, keepdims=True)
        line = line + jnp.where(lane == sub + 8 * i, whole, 0.0)
    mine = jnp.sum(line, axis=0, keepdims=True)

    def all_sum(value, source, slots, rank, size, peer, out_sem, in_sem):
        source[...] = value
        slots[rank] = value
        copies = []
        for j in range(1, size):
            to = (rank + j) % size
            copy = pltpu.make_async_remote_copy(
                src_ref=source, dst_ref=slots.at[rank], send_sem=out_sem.at[j], recv_sem=in_sem.at[j],
                device_id=peer(to), device_id_type=MESH)
            copy.start()
            copies.append(copy)
        for copy in copies:
            copy.wait()
        total = slots[0]
        for j in range(1, size):
            total = total + slots[j]
        return total

    total = all_sum(mine, partial, slots_a, rank_a, size_a, peer_a, asem, arsem)
    total = all_sum(total, mid, slots_b, rank_b, size_b, peer_b, bsem, brsem)

    def at(e):
        return jnp.broadcast_to(total[:, e:e + 1], (1, LANES))

    m = [at(e) for e in range(6)]
    h = [m[i] - m[i + 1] for i in range(5)]
    l1, l2 = h[1] / h[0], h[2] / h[0]
    d1 = h[2] - l1 * h[1]
    e1 = h[3] - l1 * h[2]
    y1 = m[1] - l1 * m[0]
    ok1 = d1 > 1e-7 * h[2]
    safe1 = jnp.where(ok1, d1, 1.0)
    l3 = e1 / safe1
    d2 = h[4] - l2 * h[2] - l3 * e1
    y2 = m[2] - l2 * m[0] - l3 * y1
    ok2 = ok1 & (d2 > 1e-7 * h[4])
    c2 = jnp.where(ok2, y2 / jnp.where(ok2, d2, 1.0), 0.0)
    c1 = jnp.where(ok1, (y1 - e1 * c2) / safe1, 0.0)
    c0 = (m[0] - h[1] * c1 - h[2] * c2) / h[0]

    rest = [1.0 - c0, c0 - c1, c1 - c2, c2]
    coef = [c0, c1, c2]
    e = 6
    closing = jnp.zeros((1, LANES), F32)
    for i in range(4):
        for j in range(i, 4):
            closing = closing + (1.0 if i == j else 2.0) * rest[i] * rest[j] * at(e)
            e += 1
    moved = jnp.zeros((1, LANES), F32)
    for i in range(3):
        for j in range(i, 3):
            moved = moved + (1.0 if i == j else 2.0) * coef[i] * coef[j] * at(e)
            e += 1
    cells = float(nz * shape_z * ny * shape_y * nt * LANES)
    norms_out[...] = jnp.sqrt(jnp.maximum(jnp.where(lane[0:1] == 0, closing, moved), 0.0) / cells)

    b0, b1, b2 = [jnp.broadcast_to(v, (ny, LANES)) for v in coef]

    @pl.loop(0, nz)
    def _(z):
        zz = z + HALO
        for t in range(nt):
            delta = b0 * u0[zz, t, own, :] + b1 * u1[zz, t, own, :] + b2 * u2[zz, t, own, :]
            press_out[z, :, pl.ds(LANES * t, LANES)] = pb[zz, t, own, :] + delta
            strain_out[z, :, pl.ds(LANES * t, LANES)] = sb[z, t] + gb[z, t] * delta


def solution(mesh):
    shape_z, shape_y = mesh.shape["gz"], mesh.shape["gy"]

    def per_device(zone_ids, fixed_cells, pressure_old, pressure_iter, strain_change, source,
                   zone_perm, zone_storage, zone_biot, zone_bulk):
        nz, ny, nx = zone_ids.shape
        nt = nx // LANES
        size_a = LINE * CORES
        size_b = shape_z * shape_y // size_a
        ext = (nz + 2 * HALO, nt, ny + 2 * TOP, LANES)
        inner = (nz, nt, ny, LANES)
        block = jax.ShapeDtypeStruct((nz, ny, nx), F32)
        dma = pltpu.SemaphoreType.DMA

        def kernel(*refs):
            body(shape_z, shape_y, nz, ny, nt, *refs)

        pressure, strain_next, norms = pl.pallas_call(
            kernel,
            out_shape=(block, block, jax.ShapeDtypeStruct((1, LANES), F32)),
            in_specs=[pl.BlockSpec(memory_space=pl.ANY)] * 6 + [pl.BlockSpec(memory_space=pltpu.SMEM)] * 4,
            out_specs=tuple([pl.BlockSpec(memory_space=pltpu.VMEM)] * 3),
            scratch_shapes=[
                pltpu.VMEM(ext, jnp.int32), pltpu.VMEM(ext, jnp.int32),
            ] + [pltpu.VMEM(ext, F32)] * 9 + [pltpu.VMEM(inner, F32)] * 6 + [
                pltpu.VMEM((1, LANES), F32), pltpu.VMEM((size_a, 1, LANES), F32),
                pltpu.VMEM((1, LANES), F32), pltpu.VMEM((size_b, 1, LANES), F32),
                dma((6, nt)), dma((32,)), dma((32,)),
                dma((size_a,)), dma((size_a,)), dma((size_b,)), dma((size_b,)),
            ],
            compiler_params=pltpu.CompilerParams(collective_id=0, has_side_effects=True),
        )(zone_ids, fixed_cells, pressure_old, pressure_iter, strain_change, source,
          zone_perm, zone_storage, zone_biot, zone_bulk)
        return pressure, strain_next, norms[0, :2]

    field = P("gz", "gy", None)
    return jax.shard_map(
        per_device, mesh=mesh,
        in_specs=(field,) * 6 + (P(),) * 4,
        out_specs=(field, field, P()),
        check_vma=False,
    )
```

time: 255 us -> 43.2 us (0.17)
  blocking collectives: 99.5 us -> 0 us
  other arithmetic: 60.5 us -> 0 us
  starting transfers between devices: 53.9 us -> 0 us
  Pallas kernels: 0 us -> 38.5 us
  waiting for transfers between devices: 18.3 us -> 0 us
  between operations: 10.6 us -> 0.65 us
  local copies, waits for them, and re-layouts: 10.1 us -> 3.89 us
    all_to_all x7 -> x0, blocking collectives: 99.5 us -> none  [copy_for_each(): lax.all_to_all(jnp.broadcast_to(array[None], (size, *array.shape)), axis,...]
    ppermute x20 -> x0, starting transfers between devices: 48.9 us -> none  [the longest x10 31.4 us: with_halo(): lax.ppermute(last, axis, up)]
    pallas_call x0 -> x1, Pallas kernels: none -> 38.5 us  [per_device(): pl.pallas_call(kernel, out_shape=(block, block, jax.ShapeDtypeStruct((1,...]
    reduce_sum x13 -> x0, other arithmetic: 26.6 us -> none  [the longest x1 14.1 us: per_device(): jnp.sum(change * change)]
    div x3 -> x0, other arithmetic: 20.7 us -> none  [per_device(): precond = residual / diagonal]
    ppermute x20 -> x0, waiting for transfers between devices: 14.5 us -> none  [the longest x10 14.5 us: with_halo(): lax.ppermute(first, axis, [(b, a) for a, b in up])]
    slice x17 -> x0, local copies, waits for them, and re-layouts: 7.97 us -> none  [the longest x3 3.22 us: in_one(): outs.append(subtotal[at:at + a.size].reshape(a.shape))]
    select_n x1 -> x0, other arithmetic: 6.78 us -> none  [lookup(): result = jnp.where(zone_ids == zone_index, zone_table[zone_index], result)]
  transfers between devices with their start and end apart: 21 -> 0, of which waited for: 5 -> 0; matrix products, arithmetic and copies ran while one was open for 5% -> 0% of each run, Pallas kernels for 0% -> 0%
where the time goes in v1:
time: 43.2 us; the launch traced here: 43.1 us
  Pallas kernels  38.5 us (89%)
  local copies, waits for them, and re-layouts  3.89 us (9%)
  between operations  0.65 us (2%)
    pallas_call x1, Pallas kernels, per_device(): pl.pallas_call(kernel, out_shape=(block, block, jax.ShapeDtypeStruct((1,...  38.5 us
    unnamed x6, local copies, waits for them, and re-layouts  3.38 us

profile of v1, /device:TPU:1, one launch (start us, length us, event | category | flops | bytes accessed | tf_op | source)
XLA Modules:
  0.0 43.1 jit_solution(16916901069949832579)
XLA Ops:
  0.6 38.5 %shard_map.121 = (f32[8,32,512]{2,1,0:T(8,128)}, f32[8,32,512]{2,1,0:T(8,128)}, f32[1,128]{1,0:T(1,128)}) custom-call(s32[8,32,512]{2,1,0:T(8,128)} %refs_0_.1, s32[8,32,512]{2,1,0:T(8,128)} %refs_1_.1, f32[8,32,512]{2,1,0:T(8,128)} %refs_2_.1, f32[8,32,512]{2,1,0:T(8,128)} %refs_3_.1, f32[8,32,512]{2,1,0:T(8,128)} %refs_4_.1, f32[8,32,512]{2,1,0:T(8,128)} %refs_5_.1, ...), custom_call_target="tpu_custom_call" | custom-call | tf_op jit(solution)/shard_map/pallas_call | solution.py:431
  39.2 0.0 copy-start.1
  39.2 0.7 %copy-done.1 = f32[1,128]{1,0:T(1,128)S(1)} copy-done((f32[1,128]{1,0:T(1,128)S(1)}, f32[1,128]{1,0:T(1,128)}, u32[]{:S(2)}) %copy-start.1) | copy-done | bytes 536
  39.8 0.5 %slice_bitcast_fusion = f32[2]{0:T(128)} fusion(f32[1,128]{1,0:T(1,128)S(1)} %copy-done.1), kind=kLoop, calls=%fused_computation | loop fusion | bytes 16 | tf_op jit(solution)/shard_map/squeeze | solution.py:447
  40.4 0.0 copy-start
  40.4 1.9 %copy.15 = f32[8,32,512]{2,1,0:T(8,128)} copy(f32[8,32,512]{2,1,0:T(8,128)} %get-tuple-element.12) | data formatting | bytes 1048576
  42.3 0.0 copy-done
  42.3 0.8 %copy.16 = f32[8,32,512]{2,1,0:T(8,128)} copy(f32[8,32,512]{2,1,0:T(8,128)S(1)} %copy-done) | data formatting | bytes 1048576
Async XLA Ops:
  39.2 0.7 %copy-start.1 = (f32[1,128]{1,0:T(1,128)S(1)}, f32[1,128]{1,0:T(1,128)}, u32[]{:S(2)}) copy-start(f32[1,128]{1,0:T(1,128)} %get-tuple-element.8) | copy-start | bytes 1540
  40.4 1.9 %copy-start = (f32[8,32,512]{2,1,0:T(8,128)S(1)}, f32[8,32,512]{2,1,0:T(8,128)}, u32[]{:S(2)}) copy-start(f32[8,32,512]{2,1,0:T(8,128)} %get-tuple-element.13) | copy-start | bytes 1572868

commit v2 on v1

v2 whole, which is shorter than its diff:
```python
import jax
import jax.numpy as jnp
from jax import lax
from jax.experimental import pallas as pl
from jax.experimental.pallas import tpu as pltpu
from jax.sharding import PartitionSpec as P

MESH = pl.DeviceIdType.MESH
F32 = jnp.float32
CORES = 2
LINE = 8
LANES = 128
HALO = 3
TOP = 8


def halo_box(side, layers_z, layers_y, nz, ny):
    def one(toward, layers, base, size):
        low, high = layers
        if toward == 0:
            return base, base, size
        if toward > 0:
            return base + low, base + size + low, high - low
        return base + size - high, base - high, high - low

    sz, dz, lz = one(side[0], layers_z, HALO, nz)
    sy, dy, ly = one(side[1], layers_y, TOP, ny)
    src = (pl.ds(sz, lz), slice(None), pl.ds(sy, ly))
    dst = (pl.ds(dz, lz), slice(None), pl.ds(dy, ly))
    return src, dst


FACES_Z = ((-1, 0), (1, 0))
FACES_Y = ((0, -1), (0, 1))
CORNERS = ((-1, -1), (-1, 1), (1, -1), (1, 1))


def pick(zone, table):
    b0 = (zone & 1) != 0
    b1 = (zone & 2) != 0
    b2 = (zone & 4) != 0

    def one(t):
        low = [jnp.where(b0, t[2 * i + 1], t[2 * i]) for i in range(4)]
        mid = [jnp.where(b1, low[2 * i + 1], low[2 * i]) for i in range(2)]
        return jnp.where(b2, mid[1], mid[0])

    return [one(t) for t in table]


def harmonic(a, b):
    return 2.0 * a * b / jnp.maximum(a + b, 1e-20)


def body(shape_z, shape_y, nz, ny, nt, zone_hbm, fixed_hbm, old_hbm, iter_hbm, strain_hbm,
         source_hbm, perm_s, stor_s, biot_s, bulk_s, press_out, strain_out, norms_out,
         zb, fb, pb, kb, fx, fy, fz, cb, u0, u1, u2, db, gb, bb, ob, sb, qb, eb, w3,
         lines, slots_a1, slots_b1, slots_a2, slots_b2,
         lsem, ssem, rsem, asem, arsem, bsem, brsem):
    gz = lax.axis_index("gz")
    gy = lax.axis_index("gy")
    chips = shape_z // CORES
    rows_y = shape_y // LINE
    my_x, my_core = gz // CORES, gz % CORES
    my_y, my_z = gy // LINE, gy % LINE
    has = {-1: (gz > 0, gy > 0), 0: (gz >= 0, gy >= 0), 1: (gz < shape_z - 1, gy < shape_y - 1)}

    def exists(side):
        return has[side[0]][0] & has[side[1]][1]

    def opposite(side):
        return (-side[0], -side[1])

    size_a = LINE * CORES
    size_b = chips * rows_y
    rank_a = my_z * CORES + my_core
    rank_b = my_y * chips + my_x

    def peer_a(rank):
        return (my_x * CORES + rank % CORES, my_y * LINE + rank // CORES)

    def peer_b(rank):
        return (rank % chips * CORES + my_core, rank // chips * LINE + my_z)

    barrier = pltpu.get_barrier_semaphore()
    expected = size_a - 1 + size_b - 1
    for side in FACES_Y + FACES_Z + CORNERS:
        expected = expected + jnp.where(exists(side), 1, 0)

        @pl.when(exists(side))
        def _():
            pl.semaphore_signal(barrier, inc=1, device_id=(gz + side[0], gy + side[1]), device_id_type=MESH)
    for j in range(1, size_a):
        pl.semaphore_signal(barrier, inc=1, device_id=peer_a((rank_a + j) % size_a), device_id_type=MESH)
    for j in range(1, size_b):
        pl.semaphore_signal(barrier, inc=1, device_id=peer_b((rank_b + j) % size_b), device_id_type=MESH)

    loads = []
    for n, (src, dst, ext) in enumerate((
        (zone_hbm, zb, True), (iter_hbm, pb, True), (fixed_hbm, fb, True),
        (old_hbm, ob, False), (strain_hbm, sb, False), (source_hbm, qb, False),
    )):
        group = []
        for t in range(nt):
            view = src.at[:, :, pl.ds(LANES * t, LANES)]
            if ext:
                into = dst.at[pl.ds(HALO, nz), t, pl.ds(TOP, ny), :]
            else:
                into = dst.at[:, t]
            copy = pltpu.make_async_copy(view, into, lsem.at[n, t])
            copy.start()
            group.append(copy)
        loads.append(group)

    own = pl.ds(TOP, ny)
    far = HALO + nz

    def clear_planes(z0):
        for t in range(nt):
            for z in range(z0, z0 + HALO):
                u0[z, t] = jnp.zeros(u0.shape[2:], F32)
                pb[z, t] = jnp.zeros(pb.shape[2:], F32)

    def clear_rows(start):
        @pl.loop(0, nz + 2 * HALO)
        def _(z):
            for t in range(nt):
                u0[z, t, pl.ds(start, TOP), :] = jnp.zeros((TOP, LANES), F32)
                pb[z, t, pl.ds(start, TOP), :] = jnp.zeros((TOP, LANES), F32)

    @pl.when(gz == 0)
    def _():
        clear_planes(0)

    @pl.when(gz == shape_z - 1)
    def _():
        clear_planes(far)

    @pl.when(gy == 0)
    def _():
        clear_rows(0)

    @pl.when(gy == shape_y - 1)
    def _():
        clear_rows(TOP + ny)

    for group in loads[:2]:
        for copy in group:
            copy.wait()
    pl.semaphore_wait(barrier, expected)

    counter = [0]
    sent = []

    def send(side, parts):
        copies = []
        for ref, layers_z, layers_y in parts:
            src, dst = halo_box(side, layers_z, layers_y, nz, ny)
            i = counter[0]
            counter[0] += 1
            copies.append(pltpu.make_async_remote_copy(
                src_ref=ref.at[src], dst_ref=ref.at[dst], send_sem=ssem.at[i], recv_sem=rsem.at[i],
                device_id=(gz - side[0], gy - side[1]), device_id_type=MESH))

        @pl.when(exists(opposite(side)))
        def _():
            for copy in copies:
                copy.start()
        sent.append((side, copies))
        return side, copies

    def receive(group):
        for side, copies in group:
            @pl.when(exists(side))
            def _():
                for copy in copies:
                    copy.wait_recv()

    one, rest, two, three = (0, 1), (1, 3), (0, 2), (0, 3)
    first = [send(side, ((pb, one, one), (zb, one, one))) for side in FACES_Y + FACES_Z]
    for copy in loads[2]:
        copy.wait()
    later = [send(side, ((zb, two, two), (fb, one, one))) for side in CORNERS]
    later += [send(side, ((zb, rest, rest), (fb, two, two))) for side in FACES_Y + FACES_Z]

    for group in loads[3:]:
        for copy in group:
            copy.wait()

    perm = [perm_s[i] for i in range(8)]
    stor = [stor_s[i] for i in range(8)]
    biot = [biot_s[i] for i in range(8)]
    gain = [biot_s[i] / bulk_s[i] for i in range(8)]
    coup = [biot[i] * biot[i] / bulk_s[i] for i in range(8)]
    keep = [stor[i] + coup[i] for i in range(8)]

    lane = lax.broadcasted_iota(jnp.int32, (8, LANES), 1)

    def x_up(tiles, wrap):
        rolled = [pltpu.roll(v, LANES - 1, 1) for v in tiles]
        last = lax.broadcasted_iota(jnp.int32, tiles[0].shape, 1) == LANES - 1
        out = []
        for t in range(nt):
            nxt = rolled[t + 1] if t + 1 < nt else (rolled[0] if wrap else jnp.zeros_like(rolled[0]))
            out.append(jnp.where(last, nxt, rolled[t]))
        return out

    def x_down(tiles):
        rolled = [pltpu.roll(v, 1, 1) for v in tiles]
        head = lax.broadcasted_iota(jnp.int32, tiles[0].shape, 1) == 0
        return [jnp.where(head, rolled[t - 1], rolled[t]) for t in range(nt)]

    def put_faces_x(z, start, size):
        rows = pl.ds(start, size)
        k = [kb[z, t, rows, :] for t in range(nt)]
        up = x_up(k, False)
        for t in range(nt):
            fx[z, t, rows, :] = harmonic(k[t], up[t])

    def put_faces_y(z, start, size):
        for t in range(nt):
            fy[z, t, pl.ds(start, size), :] = harmonic(
                kb[z, t, pl.ds(start, size), :], kb[z, t, pl.ds(start + 1, size), :])

    def put_faces_z(z, start, size):
        for t in range(nt):
            fz[z, t, pl.ds(start, size), :] = harmonic(
                kb[z, t, pl.ds(start, size), :], kb[z + 1, t, pl.ds(start, size), :])

    def diagonal(base, z, start, size):
        rows = pl.ds(start, size)
        low_x = x_down([fx[z, t, rows, :] for t in range(nt)])
        out = []
        for t in range(nt):
            d = base[t] + fz[z - 1, t, rows, :] + fz[z, t, rows, :]
            d = d + fy[z, t, pl.ds(start - 1, size), :] + fy[z, t, rows, :]
            out.append(d + low_x[t] + fx[z, t, rows, :])
        return out

    def around(src, z, start, size):
        rows, under, over = pl.ds(start, size), pl.ds(start - 1, size), pl.ds(start + 1, size)
        mid_v = [src[z, t, rows, :] for t in range(nt)]
        face = [fx[z, t, rows, :] for t in range(nt)]
        up = x_up(mid_v, True)
        down = x_down([face[t] * mid_v[t] for t in range(nt)])
        out = []
        for t in range(nt):
            total = fz[z - 1, t, rows, :] * src[z - 1, t, rows, :] + fz[z, t, rows, :] * src[z + 1, t, rows, :]
            total = total + fy[z, t, under, :] * src[z, t, under, :] + fy[z, t, rows, :] * src[z, t, over, :]
            out.append(total + down[t] + face[t] * up[t])
        return out

    def begin(z, start, size):
        rows, inner = pl.ds(start, size), pl.ds(start - TOP, size)
        diag = diagonal([eb[z - HALO, t, inner, :] for t in range(nt)], z, start, size)
        near_sum = around(pb, z, start, size)
        for t in range(nt):
            d = diag[t]
            c = (1.0 - fb[z, t, rows, :].astype(F32)) / d
            db[z - HALO, t, inner, :] = d
            cb[z, t, rows, :] = c
            u0[z, t, rows, :] = c * (bb[z - HALO, t, inner, :] - (d * pb[z, t, rows, :] - near_sum[t]))

    def advance(src, dst, z, start, size):
        rows = pl.ds(start, size)
        new = around(src, z, start, size)
        for t in range(nt):
            dst[z, t, rows, :] = cb[z, t, rows, :] * new[t]

    @pl.loop(0, nz)
    def _(z):
        for t in range(nt):
            s, a, c, g, k = pick(zb[z + HALO, t, own, :], (stor, biot, coup, gain, perm))
            kb[z + HALO, t, own, :] = k
            gb[z, t] = g
            eb[z, t] = s + c
            bb[z, t] = s * ob[z, t] + c * pb[z + HALO, t, own, :] - a * sb[z, t] + qb[z, t]

    @pl.loop(HALO, far)
    def _(z):
        put_faces_y(z, TOP, ny - 1)
        put_faces_x(z, TOP, ny)

    @pl.loop(HALO, far - 1)
    def _(z):
        put_faces_z(z, TOP, ny)

    @pl.loop(HALO + 1, far - 1)
    def _(z):
        begin(z, TOP + 1, ny - 2)

    receive(first)

    def put_perm(z, start, size, live):
        row = lax.broadcasted_iota(jnp.int32, (size, LANES), 0) + start
        inside = ((row >= TOP) | has[-1][1]) & ((row < TOP + ny) | has[1][1]) & live
        for t in range(nt):
            (k,) = pick(zb[z, t, pl.ds(start, size), :], (perm,))
            kb[z, t, pl.ds(start, size), :] = jnp.where(inside, k, 0.0)

    put_perm(HALO - 1, TOP, ny, has[-1][0])
    put_perm(far, TOP, ny, has[1][0])
    put_faces_z(HALO - 1, TOP, ny)
    put_faces_z(far - 1, TOP, ny)

    @pl.loop(HALO, far)
    def _(z):
        put_perm(z, TOP - 1, 1, has[0][0])
        put_perm(z, TOP + ny, 1, has[0][0])
        put_faces_y(z, TOP - 1, 1)
        put_faces_y(z, TOP + ny - 1, 1)

    begin(HALO, TOP, ny)
    begin(far - 1, TOP, ny)

    @pl.loop(HALO + 1, far - 1)
    def _(z):
        begin(z, TOP, 1)
        begin(z, TOP + ny - 1, 1)

    second_corners = [send(side, ((u0, two, two),)) for side in CORNERS]
    second = [send(side, ((u0, three, three),)) for side in FACES_Y + FACES_Z]

    @pl.loop(HALO + 1, far - 1)
    def _(z):
        advance(u0, u1, z, TOP + 1, ny - 2)

    receive(later)

    def put_scale(z, start, size):
        rows = pl.ds(start, size)
        base = [pick(zb[z, t, rows, :], (keep,))[0] for t in range(nt)]
        diag = diagonal(base, z, start, size)
        for t in range(nt):
            cb[z, t, rows, :] = (1.0 - fb[z, t, rows, :].astype(F32)) / diag[t]

    for z in range(HALO):
        put_perm(z, 5, 40, has[-1][0])
        put_perm(far + z, 5, 40, has[1][0])

    @pl.loop(HALO, far)
    def _(z):
        put_perm(z, 5, 3, has[0][0])
        put_perm(z, TOP + ny, 3, has[0][0])

    put_faces_z(0, 5, 40)
    for z in (1, 2, far, far + 1):
        put_faces_z(z, 5, 40)
        put_faces_y(z, 5, 38)
        put_faces_x(z, 5, 40)

    @pl.loop(HALO, far)
    def _(z):
        for start in (6, 40):
            put_faces_z(z, start, 2)
            put_faces_x(z, start, 2)
        put_faces_y(z, 5, 2)
        put_faces_y(z, 40, 2)

    for z in (1, 2, far, far + 1):
        put_scale(z, 6, 36)

    @pl.loop(HALO, far)
    def _(z):
        put_scale(z, 6, 2)
        put_scale(z, 40, 2)

    receive(second)
    receive(second_corners)

    @pl.loop(HALO + 1, far - 1)
    def _(z):
        advance(u0, u1, z, 6, 3)
        advance(u0, u1, z, 39, 3)
    for z in (HALO, far - 1):
        advance(u0, u1, z, 6, 36)
    for z in (HALO - 1, far):
        advance(u0, u1, z, 7, 34)
    for z in (HALO - 2, far + 1):
        advance(u0, u1, z, 8, 32)

    advance(u1, u2, HALO - 1, TOP, ny)
    advance(u1, u2, far, TOP, ny)

    @pl.loop(HALO, far)
    def _(z):
        advance(u1, u2, z, TOP - 1, ny + 2)

    def fold(v):
        total = v[0:8]
        for i in range(8, v.shape[0], 8):
            total = total + v[i:i + 8]
        return total

    def moment_step(z, acc):
        zz = z + HALO
        new = around(u2, zz, TOP, ny)
        acc = list(acc)
        for t in range(nt):
            d = db[z, t]
            last = (1.0 - fb[zz, t, own, :].astype(F32)) * new[t]
            w3[z, t] = last
            u = [u0[zz, t, own, :], u1[zz, t, own, :], u2[zz, t, own, :]]
            w = [d * v for v in u] + [last]
            for e, (i, j) in enumerate(((0, 0), (0, 1), (1, 1), (1, 2), (2, 2), (2, 3))):
                acc[e] = acc[e] + fold(u[i] * w[j])
        return tuple(acc)

    def norm_step(z, acc):
        zz = z + HALO
        acc = list(acc)
        for t in range(nt):
            d, g = db[z, t], gb[z, t]
            u = [u0[zz, t, own, :], u1[zz, t, own, :], u2[zz, t, own, :]]
            w = [d * v for v in u] + [w3[z, t]]
            s = [g * v for v in u]
            e = 0
            for i in range(4):
                for j in range(i, 4):
                    acc[e] = acc[e] + fold(w[i] * w[j])
                    e += 1
            for i in range(3):
                for j in range(i, 3):
                    acc[e] = acc[e] + fold(s[i] * s[j])
                    e += 1
        return tuple(acc)

    sub = lax.broadcasted_iota(jnp.int32, (8, LANES), 0)
    zero = jnp.zeros((8, LANES), F32)

    def merge(a, b, step):
        take = (sub & step) == 0
        return jnp.where(take, a, b) + pltpu.roll(jnp.where(take, b, a), step, 0)

    def in_lanes(acc):
        line = zero
        for i in range(0, len(acc), 8):
            eight = (acc[i:i + 8] + [zero] * 8)[:8]
            four = [merge(eight[j], eight[j + 1], 1) for j in range(0, 8, 2)]
            pair = [merge(four[j], four[j + 1], 2) for j in range(0, 4, 2)]
            whole = jnp.sum(merge(pair[0], pair[1], 4), axis=1, keepdims=True)
            line = line + jnp.where(lane == sub + i, whole, 0.0)
        return jnp.sum(line, axis=0, keepdims=True)

    def share(value, place, slots, rank, size, peer, out_sem, in_sem):
        lines[place] = value
        slots[rank] = value
        copies = []
        for j in range(1, size):
            copy = pltpu.make_async_remote_copy(
                src_ref=lines.at[place], dst_ref=slots.at[rank], send_sem=out_sem.at[j], recv_sem=in_sem.at[j],
                device_id=peer((rank + j) % size), device_id_type=MESH)
            copy.start()
            copies.append(copy)
        return copies

    def gather(copies, slots, size):
        for copy in copies:
            copy.wait_recv()
        total = [slots[j] for j in range(size)]
        while len(total) > 1:
            total = [total[j] + total[j + 1] for j in range(0, len(total), 2)]
        return total[0]

    acc = list(lax.fori_loop(0, nz, moment_step, (zero,) * 6))
    flight_a1 = share(in_lanes(acc), 0, slots_a1, rank_a, size_a, peer_a, asem.at[0], arsem.at[0])
    acc = list(lax.fori_loop(0, nz, norm_step, (zero,) * 16))
    flight_a2 = share(in_lanes(acc), 1, slots_a2, rank_a, size_a, peer_a, asem.at[1], arsem.at[1])
    part = gather(flight_a1, slots_a1, size_a)
    flight_b1 = share(part, 2, slots_b1, rank_b, size_b, peer_b, bsem.at[0], brsem.at[0])
    part = gather(flight_a2, slots_a2, size_a)
    flight_b2 = share(part, 3, slots_b2, rank_b, size_b, peer_b, bsem.at[1], brsem.at[1])
    total = gather(flight_b1, slots_b1, size_b)

    def at(e):
        return jnp.broadcast_to(total[:, e:e + 1], (1, LANES))

    m = [at(e) for e in range(6)]
    h = [m[i] - m[i + 1] for i in range(5)]
    l1, l2 = h[1] / h[0], h[2] / h[0]
    d1 = h[2] - l1 * h[1]
    e1 = h[3] - l1 * h[2]
    y1 = m[1] - l1 * m[0]
    ok1 = d1 > 1e-7 * h[2]
    safe1 = jnp.where(ok1, d1, 1.0)
    l3 = e1 / safe1
    d2 = h[4] - l2 * h[2] - l3 * e1
    y2 = m[2] - l2 * m[0] - l3 * y1
    ok2 = ok1 & (d2 > 1e-7 * h[4])
    c2 = jnp.where(ok2, y2 / jnp.where(ok2, d2, 1.0), 0.0)
    c1 = jnp.where(ok1, (y1 - e1 * c2) / safe1, 0.0)
    c0 = (m[0] - h[1] * c1 - h[2] * c2) / h[0]
    coef = [c0, c1, c2]

    b0, b1, b2 = [jnp.broadcast_to(v, (ny, LANES)) for v in coef]

    @pl.loop(0, nz)
    def _(z):
        zz = z + HALO
        for t in range(nt):
            delta = b0 * u0[zz, t, own, :] + b1 * u1[zz, t, own, :] + b2 * u2[zz, t, own, :]
            press_out[z, t] = pb[zz, t, own, :] + delta
            strain_out[z, t] = sb[z, t] + gb[z, t] * delta

    total = gather(flight_b2, slots_b2, size_b)
    left = [1.0 - c0, c0 - c1, c1 - c2, c2]
    e = 0
    closing = jnp.zeros((1, LANES), F32)
    for i in range(4):
        for j in range(i, 4):
            closing = closing + (1.0 if i == j else 2.0) * left[i] * left[j] * at(e)
            e += 1
    moved = jnp.zeros((1, LANES), F32)
    for i in range(3):
        for j in range(i, 3):
            moved = moved + (1.0 if i == j else 2.0) * coef[i] * coef[j] * at(e)
            e += 1
    cells = float(nz * shape_z * ny * shape_y * nt * LANES)
    norms_out[...] = jnp.sqrt(jnp.maximum(jnp.where(lane[0:1] == 0, closing, moved), 0.0) / cells)

    for side, copies in sent:
        @pl.when(exists(opposite(side)))
        def _():
            for copy in copies:
                copy.wait_send()
    for copy in flight_a1 + flight_a2 + flight_b1 + flight_b2:
        copy.wait_send()


def solution(mesh):
    shape_z, shape_y = mesh.shape["gz"], mesh.shape["gy"]

    def per_device(zone_ids, fixed_cells, pressure_old, pressure_iter, strain_change, source,
                   zone_perm, zone_storage, zone_biot, zone_bulk):
        nz, ny, nx = zone_ids.shape
        nt = nx // LANES
        size_a = LINE * CORES
        size_b = shape_z * shape_y // size_a
        ext = (nz + 2 * HALO, nt, ny + 2 * TOP, LANES)
        inner = (nz, nt, ny, LANES)
        block = jax.ShapeDtypeStruct((nz, ny, nx), F32)
        dma = pltpu.SemaphoreType.DMA

        def kernel(*refs):
            body(shape_z, shape_y, nz, ny, nt, *refs)

        results = pl.pallas_call(
            kernel,
            out_shape=(pltpu.VMEM(inner, F32), pltpu.VMEM(inner, F32), pltpu.VMEM((1, LANES), F32)),
            in_specs=[pl.BlockSpec(memory_space=pl.ANY)] * 6 + [pl.BlockSpec(memory_space=pltpu.SMEM)] * 4,
            out_specs=tuple([pl.BlockSpec(memory_space=pltpu.VMEM)] * 3),
            scratch_shapes=[
                pltpu.VMEM(ext, jnp.int32), pltpu.VMEM(ext, jnp.int32),
            ] + [pltpu.VMEM(ext, F32)] * 9 + [pltpu.VMEM(inner, F32)] * 8 + [
                pltpu.VMEM((4, 1, LANES), F32),
                pltpu.VMEM((size_a, 1, LANES), F32), pltpu.VMEM((size_b, 1, LANES), F32),
                pltpu.VMEM((size_a, 1, LANES), F32), pltpu.VMEM((size_b, 1, LANES), F32),
                dma((6, nt)), dma((40,)), dma((40,)),
                dma((2, size_a)), dma((2, size_a)), dma((2, size_b)), dma((2, size_b)),
            ],
            compiler_params=pltpu.CompilerParams(collective_id=0, has_side_effects=True),
        )(zone_ids, fixed_cells, pressure_old, pressure_iter, strain_change, source,
          zone_perm, zone_storage, zone_biot, zone_bulk)

        def emit(press_in, strain_in, norms_in, press_ref, strain_ref, norms_ref, sem):
            copies = []
            for i, (a, b) in enumerate(((press_in, press_ref), (strain_in, strain_ref))):
                for t in range(nt):
                    copy = pltpu.make_async_copy(a.at[:, t], b.at[:, :, pl.ds(LANES * t, LANES)], sem.at[i, t])
                    copy.start()
                    copies.append(copy)
            norms_ref[0] = norms_in[0, 0]
            norms_ref[1] = norms_in[0, 1]
            for copy in copies:
                copy.wait()

        return pl.pallas_call(
            emit,
            out_shape=(block, block, jax.ShapeDtypeStruct((2,), F32)),
            in_specs=[pl.BlockSpec(memory_space=pltpu.VMEM)] * 3,
            out_specs=(pl.BlockSpec(memory_space=pl.ANY),) * 2 + (pl.BlockSpec(memory_space=pltpu.SMEM),),
            scratch_shapes=[dma((2, nt))],
        )(*[pltpu.with_memory_space_constraint(v, pltpu.VMEM) for v in results])

    field = P("gz", "gy", None)
    return jax.shard_map(
        per_device, mesh=mesh,
        in_specs=(field,) * 6 + (P(),) * 4,
        out_specs=(field, field, P()),
        check_vma=False,
    )
```

time: 43.2 us -> 37.5 us (0.87)
  local copies, waits for them, and re-layouts: 3.89 us -> 0 us
  Pallas kernels: 38.5 us -> 36.8 us
    unnamed x6 -> x0, local copies, waits for them, and re-layouts: 3.38 us -> none
    pallas_call x1 -> x2, Pallas kernels: 38.5 us -> 36.8 us  [the longest x1 35.2 us: per_device(): pl.pallas_call(kernel, out_shape=(pltpu.VMEM(inner, F32), pltpu.VMEM(inne...]
    squeeze x1 -> x0, local copies, waits for them, and re-layouts: 0.51 us -> none  [per_device(): return (pressure, strain_next, norms[0, :2])]
where the time goes in v2:
time: 37.5 us; the launch traced here: 37.4 us
  Pallas kernels  36.8 us (98%)
  between operations  0.64 us (2%)
    pallas_call x1, Pallas kernels, per_device(): pl.pallas_call(kernel, out_shape=(pltpu.VMEM(inner, F32), pltpu.VMEM(inne...  35.2 us
    pallas_call x1, Pallas kernels, per_device(): pl.pallas_call(emit, out_shape=(block, block, jax.ShapeDtypeStruct((2,),...  1.55 us

profile of v2, /device:TPU:1, one launch (start us, length us, event | category | flops | bytes accessed | tf_op | source)
XLA Modules:
  0.0 37.4 jit_solution(10525579309238408814)
XLA Ops:
  0.6 35.2 %shard_map.121 = (f32[8,4,32,128]{3,2,1,0:T(8,128)S(1)}, f32[8,4,32,128]{3,2,1,0:T(8,128)S(1)}, f32[1,128]{1,0:T(1,128)S(1)}) custom-call(s32[8,32,512]{2,1,0:T(8,128)} %refs_0_.1, s32[8,32,512]{2,1,0:T(8,128)} %refs_1_.1, f32[8,32,512]{2,1,0:T(8,128)} %refs_2_.1, f32[8,32,512]{2,1,0:T(8,128)} %refs_3_.1, f32[8,32,512]{2,1,0:T(8,128)} %refs_4_.1, ...), custom_call_target="tpu_custom_call" | custom-call | tf_op jit(solution)/shard_map/pallas_call | solution.py:547
  35.9 1.5 %shard_map.122 = (f32[8,32,512]{2,1,0:T(8,128)}, f32[8,32,512]{2,1,0:T(8,128)}, f32[2]{0:T(128)}) custom-call(f32[8,4,32,128]{3,2,1,0:T(8,128)S(1)} %get-tuple-element.6.press_in, f32[8,4,32,128]{3,2,1,0:T(8,128)S(1)} %get-tuple-element.7.strain_in, f32[1,128]{1,0:T(1,128)S(1)} %get-tuple-element.8.norms_in), custom_call_target="tpu_custom_call" | custom-call | tf_op jit(solution)/shard_map/pallas_call | solution.py:577

commit v3 on v2

--- a/solution.py
+++ b/solution.py
@@ -53,10 +53,10 @@
 
 
 def body(shape_z, shape_y, nz, ny, nt, zone_hbm, fixed_hbm, old_hbm, iter_hbm, strain_hbm,
-         source_hbm, perm_s, stor_s, biot_s, bulk_s, press_out, strain_out, norms_out,
+         source_hbm, perm_hbm, stor_hbm, biot_hbm, bulk_hbm, press_out, strain_out, tail_out,
          zb, fb, pb, kb, fx, fy, fz, cb, u0, u1, u2, db, gb, bb, ob, sb, qb, eb, w3,
-         lines, slots_a1, slots_b1, slots_a2, slots_b2,
-         lsem, ssem, rsem, asem, arsem, bsem, brsem):
+         perm_s, stor_s, biot_s, bulk_s, lines, slots_a1, slots_b1, slots_a2, slots_b2,
+         tsem, lsem, ssem, rsem, asem, arsem, bsem, brsem):
     gz = lax.axis_index("gz")
     gy = lax.axis_index("gy")
     chips = shape_z // CORES
@@ -76,24 +76,27 @@
     rank_a = my_z * CORES + my_core
     rank_b = my_y * chips + my_x
 
-    def peer_a(rank):
-        return (my_x * CORES + rank % CORES, my_y * LINE + rank // CORES)
-
-    def peer_b(rank):
-        return (rank % chips * CORES + my_core, rank // chips * LINE + my_z)
+    def wrap(value, size):
+        return jnp.where(value >= size, value - size, value)
+
+    def peer_a(j):
+        return (my_x * CORES + wrap(my_core + j % CORES, CORES), my_y * LINE + wrap(my_z + j // CORES, LINE))
+
+    def peer_b(j):
+        return (wrap(my_x + j % chips, chips) * CORES + my_core, wrap(my_y + j // chips, rows_y) * LINE + my_z)
 
     barrier = pltpu.get_barrier_semaphore()
+    for j in range(1, size_a):
+        pl.semaphore_signal(barrier, inc=1, device_id=peer_a(j), device_id_type=MESH)
+    for j in range(1, size_b):
+        pl.semaphore_signal(barrier, inc=1, device_id=peer_b(j), device_id_type=MESH)
     expected = size_a - 1 + size_b - 1
-    for side in FACES_Y + FACES_Z + CORNERS:
+    for side in CORNERS + FACES_Y + FACES_Z:
         expected = expected + jnp.where(exists(side), 1, 0)
 
         @pl.when(exists(side))
         def _():
             pl.semaphore_signal(barrier, inc=1, device_id=(gz + side[0], gy + side[1]), device_id_type=MESH)
-    for j in range(1, size_a):
-        pl.semaphore_signal(barrier, inc=1, device_id=peer_a((rank_a + j) % size_a), device_id_type=MESH)
-    for j in range(1, size_b):
-        pl.semaphore_signal(barrier, inc=1, device_id=peer_b((rank_b + j) % size_b), device_id_type=MESH)
 
     loads = []
     for n, (src, dst, ext) in enumerate((
@@ -112,6 +115,12 @@
             group.append(copy)
         loads.append(group)
 
+    tables = []
+    for i, (src, dst) in enumerate(((perm_hbm, perm_s), (stor_hbm, stor_s), (biot_hbm, biot_s), (bulk_hbm, bulk_s))):
+        copy = pltpu.make_async_copy(src, dst, tsem.at[i])
+        copy.start()
+        tables.append(copy)
+
     own = pl.ds(TOP, ny)
     far = HALO + nz
 
@@ -177,7 +186,8 @@
                     copy.wait_recv()
 
     one, rest, two, three = (0, 1), (1, 3), (0, 2), (0, 3)
-    first = [send(side, ((pb, one, one), (zb, one, one))) for side in FACES_Y + FACES_Z]
+    first_y = [send(side, ((pb, one, one), (zb, one, one))) for side in FACES_Y]
+    first_z = [send(side, ((pb, one, one), (zb, one, one))) for side in FACES_Z]
     for copy in loads[2]:
         copy.wait()
     later = [send(side, ((zb, two, two), (fb, one, one))) for side in CORNERS]
@@ -187,6 +197,8 @@
         for copy in group:
             copy.wait()
 
+    for copy in tables:
+        copy.wait()
     perm = [perm_s[i] for i in range(8)]
     stor = [stor_s[i] for i in range(8)]
     biot = [biot_s[i] for i in range(8)]
@@ -289,7 +301,7 @@
     def _(z):
         begin(z, TOP + 1, ny - 2)
 
-    receive(first)
+    receive(first_z)
 
     def put_perm(z, start, size, live):
         row = lax.broadcasted_iota(jnp.int32, (size, LANES), 0) + start
@@ -303,18 +315,16 @@
     put_faces_z(HALO - 1, TOP, ny)
     put_faces_z(far - 1, TOP, ny)
 
+    begin(HALO, TOP + 1, ny - 2)
+    begin(far - 1, TOP + 1, ny - 2)
+    receive(first_y)
+
     @pl.loop(HALO, far)
     def _(z):
         put_perm(z, TOP - 1, 1, has[0][0])
         put_perm(z, TOP + ny, 1, has[0][0])
         put_faces_y(z, TOP - 1, 1)
         put_faces_y(z, TOP + ny - 1, 1)
-
-    begin(HALO, TOP, ny)
-    begin(far - 1, TOP, ny)
-
-    @pl.loop(HALO + 1, far - 1)
-    def _(z):
         begin(z, TOP, 1)
         begin(z, TOP + ny - 1, 1)
 
@@ -324,6 +334,10 @@
     @pl.loop(HALO + 1, far - 1)
     def _(z):
         advance(u0, u1, z, TOP + 1, ny - 2)
+
+    @pl.loop(HALO + 2, far - 2)
+    def _(z):
+        advance(u1, u2, z, TOP + 2, ny - 4)
 
     receive(later)
 
@@ -382,9 +396,13 @@
     advance(u1, u2, HALO - 1, TOP, ny)
     advance(u1, u2, far, TOP, ny)
 
-    @pl.loop(HALO, far)
-    def _(z):
+    for z in (HALO, HALO + 1, far - 2, far - 1):
         advance(u1, u2, z, TOP - 1, ny + 2)
+
+    @pl.loop(HALO + 2, far - 2)
+    def _(z):
+        advance(u1, u2, z, TOP - 1, 3)
+        advance(u1, u2, z, TOP + ny - 2, 3)
 
     def fold(v):
         total = v[0:8]
@@ -449,7 +467,7 @@
         for j in range(1, size):
             copy = pltpu.make_async_remote_copy(
                 src_ref=lines.at[place], dst_ref=slots.at[rank], send_sem=out_sem.at[j], recv_sem=in_sem.at[j],
-                device_id=peer((rank + j) % size), device_id_type=MESH)
+                device_id=peer(j), device_id_type=MESH)
             copy.start()
             copies.append(copy)
         return copies
@@ -466,10 +484,17 @@
     flight_a1 = share(in_lanes(acc), 0, slots_a1, rank_a, size_a, peer_a, asem.at[0], arsem.at[0])
     acc = list(lax.fori_loop(0, nz, norm_step, (zero,) * 16))
     flight_a2 = share(in_lanes(acc), 1, slots_a2, rank_a, size_a, peer_a, asem.at[1], arsem.at[1])
+    for side, copies in sent:
+        @pl.when(exists(opposite(side)))
+        def _():
+            for copy in copies:
+                copy.wait_send()
     part = gather(flight_a1, slots_a1, size_a)
     flight_b1 = share(part, 2, slots_b1, rank_b, size_b, peer_b, bsem.at[0], brsem.at[0])
     part = gather(flight_a2, slots_a2, size_a)
     flight_b2 = share(part, 3, slots_b2, rank_b, size_b, peer_b, bsem.at[1], brsem.at[1])
+    for copy in flight_a1 + flight_a2:
+        copy.wait_send()
     total = gather(flight_b1, slots_b1, size_b)
 
     def at(e):
@@ -499,32 +524,33 @@
         zz = z + HALO
         for t in range(nt):
             delta = b0 * u0[zz, t, own, :] + b1 * u1[zz, t, own, :] + b2 * u2[zz, t, own, :]
-            press_out[z, t] = pb[zz, t, own, :] + delta
-            strain_out[z, t] = sb[z, t] + gb[z, t] * delta
-
-    total = gather(flight_b2, slots_b2, size_b)
-    left = [1.0 - c0, c0 - c1, c1 - c2, c2]
+            press_out[z, :, pl.ds(LANES * t, LANES)] = pb[zz, t, own, :] + delta
+            strain_out[z, :, pl.ds(LANES * t, LANES)] = sb[z, t] + gb[z, t] * delta
+
+    for copy in flight_b1 + flight_b2:
+        copy.wait_send()
+    tail_out[0:1, :] = gather(flight_b2, slots_b2, size_b)
+    for i in range(3):
+        tail_out[i + 1:i + 2, :] = coef[i]
+
+
+def norms(tail, cells):
+    def at(e):
+        return jnp.broadcast_to(tail[0:1, e:e + 1], (1, LANES))
+
+    c = [tail[i:i + 1] for i in range(1, 4)]
+    left = [1.0 - c[0], c[0] - c[1], c[1] - c[2], c[2]]
     e = 0
-    closing = jnp.zeros((1, LANES), F32)
-    for i in range(4):
-        for j in range(i, 4):
-            closing = closing + (1.0 if i == j else 2.0) * left[i] * left[j] * at(e)
-            e += 1
-    moved = jnp.zeros((1, LANES), F32)
-    for i in range(3):
-        for j in range(i, 3):
-            moved = moved + (1.0 if i == j else 2.0) * coef[i] * coef[j] * at(e)
-            e += 1
-    cells = float(nz * shape_z * ny * shape_y * nt * LANES)
-    norms_out[...] = jnp.sqrt(jnp.maximum(jnp.where(lane[0:1] == 0, closing, moved), 0.0) / cells)
-
-    for side, copies in sent:
-        @pl.when(exists(opposite(side)))
-        def _():
-            for copy in copies:
-                copy.wait_send()
-    for copy in flight_a1 + flight_a2 + flight_b1 + flight_b2:
-        copy.wait_send()
+    out = []
+    for v in (left, c):
+        total = jnp.zeros((1, LANES), F32)
+        for i in range(len(v)):
+            for j in range(i, len(v)):
+                total = total + (1.0 if i == j else 2.0) * v[i] * v[j] * at(e)
+                e += 1
+        out.append(total)
+    lane = lax.broadcasted_iota(jnp.int32, (1, LANES), 1)
+    return jnp.sqrt(jnp.maximum(jnp.where(lane == 0, out[0], out[1]), 0.0) / cells)
 
 
 def solution(mesh):
@@ -546,31 +572,36 @@
 
         results = pl.pallas_call(
             kernel,
-            out_shape=(pltpu.VMEM(inner, F32), pltpu.VMEM(inner, F32), pltpu.VMEM((1, LANES), F32)),
-            in_specs=[pl.BlockSpec(memory_space=pl.ANY)] * 6 + [pl.BlockSpec(memory_space=pltpu.SMEM)] * 4,
+            out_shape=(pltpu.VMEM((nz, ny, nx), F32), pltpu.VMEM((nz, ny, nx), F32), pltpu.VMEM((8, LANES), F32)),
+            in_specs=[pl.BlockSpec(memory_space=pl.ANY)] * 10,
             out_specs=tuple([pl.BlockSpec(memory_space=pltpu.VMEM)] * 3),
             scratch_shapes=[
                 pltpu.VMEM(ext, jnp.int32), pltpu.VMEM(ext, jnp.int32),
             ] + [pltpu.VMEM(ext, F32)] * 9 + [pltpu.VMEM(inner, F32)] * 8 + [
+                pltpu.SMEM((8,), F32), pltpu.SMEM((8,), F32), pltpu.SMEM((8,), F32), pltpu.SMEM((8,), F32),
                 pltpu.VMEM((4, 1, LANES), F32),
                 pltpu.VMEM((size_a, 1, LANES), F32), pltpu.VMEM((size_b, 1, LANES), F32),
                 pltpu.VMEM((size_a, 1, LANES), F32), pltpu.VMEM((size_b, 1, LANES), F32),
-                dma((6, nt)), dma((40,)), dma((40,)),
+                dma((4,)), dma((6, nt)), dma((40,)), dma((40,)),
                 dma((2, size_a)), dma((2, size_a)), dma((2, size_b)), dma((2, size_b)),
             ],
             compiler_params=pltpu.CompilerParams(collective_id=0, has_side_effects=True),
         )(zone_ids, fixed_cells, pressure_old, pressure_iter, strain_change, source,
           zone_perm, zone_storage, zone_biot, zone_bulk)
 
-        def emit(press_in, strain_in, norms_in, press_ref, strain_ref, norms_ref, sem):
+        cells = float(nz * shape_z * ny * shape_y * nx)
+
+        def emit(press_in, strain_in, tail_in, press_ref, strain_ref, norms_ref, sem):
             copies = []
             for i, (a, b) in enumerate(((press_in, press_ref), (strain_in, strain_ref))):
-                for t in range(nt):
-                    copy = pltpu.make_async_copy(a.at[:, t], b.at[:, :, pl.ds(LANES * t, LANES)], sem.at[i, t])
+                for j in range(4):
+                    part = pl.ds(j * nz // 4, nz // 4)
+                    copy = pltpu.make_async_copy(a.at[part], b.at[part], sem.at[i, j])
                     copy.start()
                     copies.append(copy)
-            norms_ref[0] = norms_in[0, 0]
-            norms_ref[1] = norms_in[0, 1]
+            both = norms(tail_in[...], cells)
+            norms_ref[0] = both[0, 0]
+            norms_ref[1] = both[0, 1]
             for copy in copies:
                 copy.wait()
 
@@ -579,7 +610,7 @@
             out_shape=(block, block, jax.ShapeDtypeStruct((2,), F32)),
             in_specs=[pl.BlockSpec(memory_space=pltpu.VMEM)] * 3,
             out_specs=(pl.BlockSpec(memory_space=pl.ANY),) * 2 + (pl.BlockSpec(memory_space=pltpu.SMEM),),
-            scratch_shapes=[dma((2, nt))],
+            scratch_shapes=[dma((2, 4))],
         )(*[pltpu.with_memory_space_constraint(v, pltpu.VMEM) for v in results])
 
     field = P("gz", "gy", None)

time: 37.5 us -> 35.8 us (0.955)
  Pallas kernels: 36.8 us -> 35.1 us
    pallas_call x1, Pallas kernels: 35.2 us -> 33.5 us  [per_device(): pl.pallas_call(kernel, out_shape=(pltpu.VMEM((nz, ny, nx), F32), pltpu.VM...]
where the time goes in v3:
time: 35.8 us; the launch traced here: 35.7 us
  Pallas kernels  35.1 us (98%)
  between operations  0.64 us (2%)
    pallas_call x1, Pallas kernels, per_device(): pl.pallas_call(kernel, out_shape=(pltpu.VMEM((nz, ny, nx), F32), pltpu.VM...  33.5 us
    pallas_call x1, Pallas kernels, per_device(): pl.pallas_call(emit, out_shape=(block, block, jax.ShapeDtypeStruct((2,),...  1.54 us

profile of v3, /device:TPU:1, one launch (start us, length us, event | category | flops | bytes accessed | tf_op | source)
XLA Modules:
  0.0 35.7 jit_solution(672835863410047596)
XLA Ops:
  0.6 33.5 %shard_map.121 = (f32[8,32,512]{2,1,0:T(8,128)S(1)}, f32[8,32,512]{2,1,0:T(8,128)S(1)}, f32[8,128]{1,0:T(8,128)S(1)}) custom-call(s32[8,32,512]{2,1,0:T(8,128)} %refs_0_.1, s32[8,32,512]{2,1,0:T(8,128)} %refs_1_.1, f32[8,32,512]{2,1,0:T(8,128)} %refs_2_.1, f32[8,32,512]{2,1,0:T(8,128)} %refs_3_.1, f32[8,32,512]{2,1,0:T(8,128)} %refs_4_.1, ...), custom_call_target="tpu_custom_call" | custom-call | tf_op jit(solution)/shard_map/pallas_call | solution.py:573
  34.2 1.5 %shard_map.122 = (f32[8,32,512]{2,1,0:T(8,128)}, f32[8,32,512]{2,1,0:T(8,128)}, f32[2]{0:T(128)}) custom-call(f32[8,32,512]{2,1,0:T(8,128)S(1)} %get-tuple-element.6.press_in, f32[8,32,512]{2,1,0:T(8,128)S(1)} %get-tuple-element.7.strain_in, f32[8,128]{1,0:T(8,128)S(1)} %get-tuple-element.8.tail_in), custom_call_target="tpu_custom_call" | custom-call | tf_op jit(solution)/shard_map/pallas_call | solution.py:608

commit v4 on v3

--- a/solution.py
+++ b/solution.py
@@ -103,17 +103,15 @@
         (zone_hbm, zb, True), (iter_hbm, pb, True), (fixed_hbm, fb, True),
         (old_hbm, ob, False), (strain_hbm, sb, False), (source_hbm, qb, False),
     )):
-        group = []
         for t in range(nt):
             view = src.at[:, :, pl.ds(LANES * t, LANES)]
             if ext:
                 into = dst.at[pl.ds(HALO, nz), t, pl.ds(TOP, ny), :]
             else:
                 into = dst.at[:, t]
-            copy = pltpu.make_async_copy(view, into, lsem.at[n, t])
-            copy.start()
-            group.append(copy)
-        loads.append(group)
+            pltpu.make_async_copy(view, into, lsem.at[n]).start()
+        whole = dst.at[pl.ds(HALO, nz), :, pl.ds(TOP, ny), :] if ext else dst
+        loads.append([pltpu.make_async_copy(whole, whole, lsem.at[n])])
 
     tables = []
     for i, (src, dst) in enumerate(((perm_hbm, perm_s), (stor_hbm, stor_s), (biot_hbm, biot_s), (bulk_hbm, bulk_s))):
@@ -319,12 +317,12 @@
     begin(far - 1, TOP + 1, ny - 2)
     receive(first_y)
 
-    @pl.loop(HALO, far)
-    def _(z):
+    for z in range(HALO, far):
         put_perm(z, TOP - 1, 1, has[0][0])
         put_perm(z, TOP + ny, 1, has[0][0])
         put_faces_y(z, TOP - 1, 1)
         put_faces_y(z, TOP + ny - 1, 1)
+    for z in range(HALO, far):
         begin(z, TOP, 1)
         begin(z, TOP + ny - 1, 1)
 
@@ -382,8 +380,7 @@
     receive(second)
     receive(second_corners)
 
-    @pl.loop(HALO + 1, far - 1)
-    def _(z):
+    for z in range(HALO + 1, far - 1):
         advance(u0, u1, z, 6, 3)
         advance(u0, u1, z, 39, 3)
     for z in (HALO, far - 1):
@@ -399,8 +396,7 @@
     for z in (HALO, HALO + 1, far - 2, far - 1):
         advance(u1, u2, z, TOP - 1, ny + 2)
 
-    @pl.loop(HALO + 2, far - 2)
-    def _(z):
+    for z in range(HALO + 2, far - 2):
         advance(u1, u2, z, TOP - 1, 3)
         advance(u1, u2, z, TOP + ny - 2, 3)
 
@@ -463,24 +459,23 @@
     def share(value, place, slots, rank, size, peer, out_sem, in_sem):
         lines[place] = value
         slots[rank] = value
-        copies = []
         for j in range(1, size):
-            copy = pltpu.make_async_remote_copy(
-                src_ref=lines.at[place], dst_ref=slots.at[rank], send_sem=out_sem.at[j], recv_sem=in_sem.at[j],
-                device_id=peer(j), device_id_type=MESH)
-            copy.start()
-            copies.append(copy)
-        return copies
-
-    def gather(copies, slots, size):
-        for copy in copies:
-            copy.wait_recv()
+            pltpu.make_async_remote_copy(
+                src_ref=lines.at[place], dst_ref=slots.at[rank], send_sem=out_sem, recv_sem=in_sem,
+                device_id=peer(j), device_id_type=MESH).start()
+        all_of = slots.at[pl.ds(0, size - 1)]
+        return pltpu.make_async_remote_copy(
+            src_ref=all_of, dst_ref=all_of, send_sem=out_sem, recv_sem=in_sem,
+            device_id=peer(1), device_id_type=MESH)
+
+    def gather(flight, slots, size):
+        flight.wait_recv()
         total = [slots[j] for j in range(size)]
         while len(total) > 1:
             total = [total[j] + total[j + 1] for j in range(0, len(total), 2)]
         return total[0]
 
-    acc = list(lax.fori_loop(0, nz, moment_step, (zero,) * 6))
+    acc = list(lax.fori_loop(0, nz // 2, lambda i, a: moment_step(2 * i + 1, moment_step(2 * i, a)), (zero,) * 6))
     flight_a1 = share(in_lanes(acc), 0, slots_a1, rank_a, size_a, peer_a, asem.at[0], arsem.at[0])
     acc = list(lax.fori_loop(0, nz, norm_step, (zero,) * 16))
     flight_a2 = share(in_lanes(acc), 1, slots_a2, rank_a, size_a, peer_a, asem.at[1], arsem.at[1])
@@ -493,8 +488,8 @@
     flight_b1 = share(part, 2, slots_b1, rank_b, size_b, peer_b, bsem.at[0], brsem.at[0])
     part = gather(flight_a2, slots_a2, size_a)
     flight_b2 = share(part, 3, slots_b2, rank_b, size_b, peer_b, bsem.at[1], brsem.at[1])
-    for copy in flight_a1 + flight_a2:
-        copy.wait_send()
+    flight_a1.wait_send()
+    flight_a2.wait_send()
     total = gather(flight_b1, slots_b1, size_b)
 
     def at(e):
@@ -527,8 +522,8 @@
             press_out[z, :, pl.ds(LANES * t, LANES)] = pb[zz, t, own, :] + delta
             strain_out[z, :, pl.ds(LANES * t, LANES)] = sb[z, t] + gb[z, t] * delta
 
-    for copy in flight_b1 + flight_b2:
-        copy.wait_send()
+    flight_b1.wait_send()
+    flight_b2.wait_send()
     tail_out[0:1, :] = gather(flight_b2, slots_b2, size_b)
     for i in range(3):
         tail_out[i + 1:i + 2, :] = coef[i]
@@ -582,8 +577,8 @@
                 pltpu.VMEM((4, 1, LANES), F32),
                 pltpu.VMEM((size_a, 1, LANES), F32), pltpu.VMEM((size_b, 1, LANES), F32),
                 pltpu.VMEM((size_a, 1, LANES), F32), pltpu.VMEM((size_b, 1, LANES), F32),
-                dma((4,)), dma((6, nt)), dma((40,)), dma((40,)),
-                dma((2, size_a)), dma((2, size_a)), dma((2, size_b)), dma((2, size_b)),
+                dma((4,)), dma((6,)), dma((32,)), dma((32,)),
+                dma((2,)), dma((2,)), dma((2,)), dma((2,)),
             ],
             compiler_params=pltpu.CompilerParams(collective_id=0, has_side_effects=True),
         )(zone_ids, fixed_cells, pressure_old, pressure_iter, strain_change, source,

time: 35.8 us -> 33.2 us (0.927)
  Pallas kernels: 35.1 us -> 32.5 us
    pallas_call x1, Pallas kernels: 33.5 us -> 30.9 us  [per_device(): pl.pallas_call(kernel, out_shape=(pltpu.VMEM((nz, ny, nx), F32), pltpu.VM...]
where the time goes in v4:
time: 33.2 us; the launch traced here: 33.1 us
  Pallas kernels  32.5 us (98%)
  between operations  0.64 us (2%)
    pallas_call x1, Pallas kernels, per_device(): pl.pallas_call(kernel, out_shape=(pltpu.VMEM((nz, ny, nx), F32), pltpu.VM...  30.9 us
    pallas_call x1, Pallas kernels, per_device(): pl.pallas_call(emit, out_shape=(block, block, jax.ShapeDtypeStruct((2,),...  1.54 us

profile of v4, /device:TPU:1, one launch (start us, length us, event | category | flops | bytes accessed | tf_op | source)
XLA Modules:
  0.0 33.1 jit_solution(15430399978038790588)
XLA Ops:
  0.6 30.9 %shard_map.121 = (f32[8,32,512]{2,1,0:T(8,128)S(1)}, f32[8,32,512]{2,1,0:T(8,128)S(1)}, f32[8,128]{1,0:T(8,128)S(1)}) custom-call(s32[8,32,512]{2,1,0:T(8,128)} %refs_0_.1, s32[8,32,512]{2,1,0:T(8,128)} %refs_1_.1, f32[8,32,512]{2,1,0:T(8,128)} %refs_2_.1, f32[8,32,512]{2,1,0:T(8,128)} %refs_3_.1, f32[8,32,512]{2,1,0:T(8,128)} %refs_4_.1, ...), custom_call_target="tpu_custom_call" | custom-call | tf_op jit(solution)/shard_map/pallas_call | solution.py:568
  31.6 1.5 %shard_map.122 = (f32[8,32,512]{2,1,0:T(8,128)}, f32[8,32,512]{2,1,0:T(8,128)}, f32[2]{0:T(128)}) custom-call(f32[8,32,512]{2,1,0:T(8,128)S(1)} %get-tuple-element.6.press_in, f32[8,32,512]{2,1,0:T(8,128)S(1)} %get-tuple-element.7.strain_in, f32[8,128]{1,0:T(8,128)S(1)} %get-tuple-element.8.tail_in), custom_call_target="tpu_custom_call" | custom-call | tf_op jit(solution)/shard_map/pallas_call | solution.py:603

commit v5 on v4

--- a/solution.py
+++ b/solution.py
@@ -33,6 +33,7 @@
 FACES_Z = ((-1, 0), (1, 0))
 FACES_Y = ((0, -1), (0, 1))
 CORNERS = ((-1, -1), (-1, 1), (1, -1), (1, 1))
+ALL = FACES_Z + FACES_Y + CORNERS
 
 
 def pick(zone, table):
@@ -157,31 +158,41 @@
     pl.semaphore_wait(barrier, expected)
 
     counter = [0]
-    sent = []
+    sent = {}
 
     def send(side, parts):
-        copies = []
+        i = counter[0]
+        counter[0] += 1
+        sems = dict(send_sem=ssem.at[ALL.index(side)], recv_sem=rsem.at[i],
+                    device_id=(gz - side[0], gy - side[1]), device_id_type=MESH)
+        copies, units = [], 0
         for ref, layers_z, layers_y in parts:
             src, dst = halo_box(side, layers_z, layers_y, nz, ny)
-            i = counter[0]
-            counter[0] += 1
-            copies.append(pltpu.make_async_remote_copy(
-                src_ref=ref.at[src], dst_ref=ref.at[dst], send_sem=ssem.at[i], recv_sem=rsem.at[i],
-                device_id=(gz - side[0], gy - side[1]), device_id_type=MESH))
+            copies.append(pltpu.make_async_remote_copy(src_ref=ref.at[src], dst_ref=ref.at[dst], **sems))
+            wide, tall = layers_z[1] - layers_z[0], layers_y[1] - layers_y[0]
+            units += (wide if side[0] else 1) * (tall if side[1] else 1)
 
         @pl.when(exists(opposite(side)))
         def _():
             for copy in copies:
                 copy.start()
-        sent.append((side, copies))
-        return side, copies
+        sent[side] = sent.get(side, 0) + units
+        return side, units, sems
+
+    def bytes_of(side, units, sems):
+        if side[1] == 0:
+            box = pb.at[pl.ds(0, units), :, own, :]
+        elif side[0] == 0:
+            box = pb.at[pl.ds(HALO, nz), :, pl.ds(0, units), :]
+        else:
+            box = pb.at[pl.ds(0, units), :, pl.ds(0, 1), :]
+        return pltpu.make_async_remote_copy(src_ref=box, dst_ref=box, **sems)
 
     def receive(group):
-        for side, copies in group:
+        for side, units, sems in group:
             @pl.when(exists(side))
             def _():
-                for copy in copies:
-                    copy.wait_recv()
+                bytes_of(side, units, sems).wait_recv()
 
     one, rest, two, three = (0, 1), (1, 3), (0, 2), (0, 3)
     first_y = [send(side, ((pb, one, one), (zb, one, one))) for side in FACES_Y]
@@ -479,11 +490,10 @@
     flight_a1 = share(in_lanes(acc), 0, slots_a1, rank_a, size_a, peer_a, asem.at[0], arsem.at[0])
     acc = list(lax.fori_loop(0, nz, norm_step, (zero,) * 16))
     flight_a2 = share(in_lanes(acc), 1, slots_a2, rank_a, size_a, peer_a, asem.at[1], arsem.at[1])
-    for side, copies in sent:
+    for side, units, sems in second + second_corners:
         @pl.when(exists(opposite(side)))
         def _():
-            for copy in copies:
-                copy.wait_send()
+            bytes_of(side, sent[side], sems).wait_send()
     part = gather(flight_a1, slots_a1, size_a)
     flight_b1 = share(part, 2, slots_b1, rank_b, size_b, peer_b, bsem.at[0], brsem.at[0])
     part = gather(flight_a2, slots_a2, size_a)
@@ -577,7 +587,7 @@
                 pltpu.VMEM((4, 1, LANES), F32),
                 pltpu.VMEM((size_a, 1, LANES), F32), pltpu.VMEM((size_b, 1, LANES), F32),
                 pltpu.VMEM((size_a, 1, LANES), F32), pltpu.VMEM((size_b, 1, LANES), F32),
-                dma((4,)), dma((6,)), dma((32,)), dma((32,)),
+                dma((4,)), dma((6,)), dma((8,)), dma((20,)),
                 dma((2,)), dma((2,)), dma((2,)), dma((2,)),
             ],
             compiler_params=pltpu.CompilerParams(collective_id=0, has_side_effects=True),
@@ -586,7 +596,7 @@
 
         cells = float(nz * shape_z * ny * shape_y * nx)
 
-        def emit(press_in, strain_in, tail_in, press_ref, strain_ref, norms_ref, sem):
+        def emit(press_in, strain_in, tail_in, press_ref, strain_ref, norms_ref, pair, sem, pair_sem):
             copies = []
             for i, (a, b) in enumerate(((press_in, press_ref), (strain_in, strain_ref))):
                 for j in range(4):
@@ -595,8 +605,11 @@
                     copy.start()
                     copies.append(copy)
             both = norms(tail_in[...], cells)
-            norms_ref[0] = both[0, 0]
-            norms_ref[1] = both[0, 1]
+            pair[0] = both[0, 0]
+            pair[1] = both[0, 1]
+            copy = pltpu.make_async_copy(pair, norms_ref, pair_sem)
+            copy.start()
+            copies.append(copy)
             for copy in copies:
                 copy.wait()
 
@@ -604,8 +617,8 @@
             emit,
             out_shape=(block, block, jax.ShapeDtypeStruct((2,), F32)),
             in_specs=[pl.BlockSpec(memory_space=pltpu.VMEM)] * 3,
-            out_specs=(pl.BlockSpec(memory_space=pl.ANY),) * 2 + (pl.BlockSpec(memory_space=pltpu.SMEM),),
-            scratch_shapes=[dma((2, 4))],
+            out_specs=(pl.BlockSpec(memory_space=pl.ANY),) * 3,
+            scratch_shapes=[pltpu.SMEM((2,), F32), dma((2, 4)), dma],
         )(*[pltpu.with_memory_space_constraint(v, pltpu.VMEM) for v in results])
 
     field = P("gz", "gy", None)

time: 33.2 us -> 32.4 us (0.976)
  Pallas kernels: 32.5 us -> 31.6 us
    pallas_call x1, Pallas kernels: 1.54 us -> 1.05 us  [per_device(): pl.pallas_call(emit, out_shape=(block, block, jax.ShapeDtypeStruct((2,),...]
where the time goes in v5:
time: 32.4 us; the launch traced here: 32.3 us
  Pallas kernels  31.6 us (98%)
  between operations  0.64 us (2%)
    pallas_call x1, Pallas kernels, per_device(): pl.pallas_call(kernel, out_shape=(pltpu.VMEM((nz, ny, nx), F32), pltpu.VM...  30.6 us
    pallas_call x1, Pallas kernels, per_device(): pl.pallas_call(emit, out_shape=(block, block, jax.ShapeDtypeStruct((2,),...  1.05 us

profile of v5, /device:TPU:1, one launch (start us, length us, event | category | flops | bytes accessed | tf_op | source)
XLA Modules:
  0.0 32.3 jit_solution(14108719669863906227)
XLA Ops:
  0.6 30.6 %shard_map.121 = (f32[8,32,512]{2,1,0:T(8,128)S(1)}, f32[8,32,512]{2,1,0:T(8,128)S(1)}, f32[8,128]{1,0:T(8,128)S(1)}) custom-call(s32[8,32,512]{2,1,0:T(8,128)} %refs_0_.1, s32[8,32,512]{2,1,0:T(8,128)} %refs_1_.1, f32[8,32,512]{2,1,0:T(8,128)} %refs_2_.1, f32[8,32,512]{2,1,0:T(8,128)} %refs_3_.1, f32[8,32,512]{2,1,0:T(8,128)} %refs_4_.1, ...), custom_call_target="tpu_custom_call" | custom-call | tf_op jit(solution)/shard_map/pallas_call | solution.py:578
  31.2 1.0 %shard_map.122 = (f32[8,32,512]{2,1,0:T(8,128)}, f32[8,32,512]{2,1,0:T(8,128)}, f32[2]{0:T(128)}) custom-call(f32[8,32,512]{2,1,0:T(8,128)S(1)} %get-tuple-element.6.press_in, f32[8,32,512]{2,1,0:T(8,128)S(1)} %get-tuple-element.7.strain_in, f32[8,128]{1,0:T(8,128)S(1)} %get-tuple-element.8.tail_in), custom_call_target="tpu_custom_call" | custom-call | tf_op jit(solution)/shard_map/pallas_call | solution.py:616

commit v6 on v5

--- a/solution.py
+++ b/solution.py
@@ -348,6 +348,24 @@
     def _(z):
         advance(u1, u2, z, TOP + 2, ny - 4)
 
+    def fold(v):
+        total = v[0:8]
+        for i in range(8, v.shape[0], 8):
+            total = total + v[i:i + 8]
+        return total
+
+    def early_step(z, acc):
+        acc = list(acc)
+        for t in range(nt):
+            u = u0[z + HALO, t, own, :]
+            w, s = db[z, t] * u, gb[z, t] * u
+            for e, (a, b) in enumerate(((u, w), (w, w), (s, s))):
+                acc[e] = acc[e] + fold(a * b)
+        return tuple(acc)
+
+    zero = jnp.zeros((8, LANES), F32)
+    early = lax.fori_loop(0, nz, early_step, (zero,) * 3)
+
     receive(later)
 
     def put_scale(z, start, size):
@@ -411,12 +429,6 @@
         advance(u1, u2, z, TOP - 1, 3)
         advance(u1, u2, z, TOP + ny - 2, 3)
 
-    def fold(v):
-        total = v[0:8]
-        for i in range(8, v.shape[0], 8):
-            total = total + v[i:i + 8]
-        return total
-
     def moment_step(z, acc):
         zz = z + HALO
         new = around(u2, zz, TOP, ny)
@@ -427,7 +439,7 @@
             w3[z, t] = last
             u = [u0[zz, t, own, :], u1[zz, t, own, :], u2[zz, t, own, :]]
             w = [d * v for v in u] + [last]
-            for e, (i, j) in enumerate(((0, 0), (0, 1), (1, 1), (1, 2), (2, 2), (2, 3))):
+            for e, (i, j) in enumerate(((0, 1), (1, 1), (1, 2), (2, 2), (2, 3))):
                 acc[e] = acc[e] + fold(u[i] * w[j])
         return tuple(acc)
 
@@ -441,17 +453,16 @@
             s = [g * v for v in u]
             e = 0
             for i in range(4):
-                for j in range(i, 4):
+                for j in range(max(i, 1), 4):
                     acc[e] = acc[e] + fold(w[i] * w[j])
                     e += 1
             for i in range(3):
-                for j in range(i, 3):
+                for j in range(max(i, 1), 3):
                     acc[e] = acc[e] + fold(s[i] * s[j])
                     e += 1
         return tuple(acc)
 
     sub = lax.broadcasted_iota(jnp.int32, (8, LANES), 0)
-    zero = jnp.zeros((8, LANES), F32)
 
     def merge(a, b, step):
         take = (sub & step) == 0
@@ -486,9 +497,11 @@
             total = [total[j] + total[j + 1] for j in range(0, len(total), 2)]
         return total[0]
 
-    acc = list(lax.fori_loop(0, nz // 2, lambda i, a: moment_step(2 * i + 1, moment_step(2 * i, a)), (zero,) * 6))
+    acc = list(lax.fori_loop(0, nz // 2, lambda i, a: moment_step(2 * i + 1, moment_step(2 * i, a)), (zero,) * 5))
+    acc = [early[0]] + acc
     flight_a1 = share(in_lanes(acc), 0, slots_a1, rank_a, size_a, peer_a, asem.at[0], arsem.at[0])
-    acc = list(lax.fori_loop(0, nz, norm_step, (zero,) * 16))
+    acc = list(lax.fori_loop(0, nz, norm_step, (zero,) * 14))
+    acc = [early[1]] + acc[:9] + [early[2]] + acc[9:]
     flight_a2 = share(in_lanes(acc), 1, slots_a2, rank_a, size_a, peer_a, asem.at[1], arsem.at[1])
     for side, units, sems in second + second_corners:
         @pl.when(exists(opposite(side)))

time: 32.4 us -> 32.3 us (level)
  no operation moved by 1% of the time
where the time goes in v6:
time: 32.3 us; the launch traced here: 32.2 us
  Pallas kernels  31.5 us (98%)
  between operations  0.64 us (2%)
    pallas_call x1, Pallas kernels, per_device(): pl.pallas_call(kernel, out_shape=(pltpu.VMEM((nz, ny, nx), F32), pltpu.VM...  30.5 us
    pallas_call x1, Pallas kernels, per_device(): pl.pallas_call(emit, out_shape=(block, block, jax.ShapeDtypeStruct((2,),...  1.05 us

profile of v6, /device:TPU:1, one launch (start us, length us, event | category | flops | bytes accessed | tf_op | source)
XLA Modules:
  0.0 32.2 jit_solution(17966225239050005278)
XLA Ops:
  0.6 30.5 %shard_map.121 = (f32[8,32,512]{2,1,0:T(8,128)S(1)}, f32[8,32,512]{2,1,0:T(8,128)S(1)}, f32[8,128]{1,0:T(8,128)S(1)}) custom-call(s32[8,32,512]{2,1,0:T(8,128)} %refs_0_.1, s32[8,32,512]{2,1,0:T(8,128)} %refs_1_.1, f32[8,32,512]{2,1,0:T(8,128)} %refs_2_.1, f32[8,32,512]{2,1,0:T(8,128)} %refs_3_.1, f32[8,32,512]{2,1,0:T(8,128)} %refs_4_.1, ...), custom_call_target="tpu_custom_call" | custom-call | tf_op jit(solution)/shard_map/pallas_call | solution.py:591
  31.1 1.0 %shard_map.122 = (f32[8,32,512]{2,1,0:T(8,128)}, f32[8,32,512]{2,1,0:T(8,128)}, f32[2]{0:T(128)}) custom-call(f32[8,32,512]{2,1,0:T(8,128)S(1)} %get-tuple-element.6.press_in, f32[8,32,512]{2,1,0:T(8,128)S(1)} %get-tuple-element.7.strain_in, f32[8,128]{1,0:T(8,128)S(1)} %get-tuple-element.8.tail_in), custom_call_target="tpu_custom_call" | custom-call | tf_op jit(solution)/shard_map/pallas_call | solution.py:629
